TPU v7x, 128 devices: a whole 4x4x4 slice. The times are simulated.
128 devices in a mesh: row: 8 (over x, y_hi), col: 16 (over y_lo, z, core).
Axes of the slice: x: 4, y: 4 (y_hi: 2, y_lo: 2; y = y_hi * 2 + y_lo), z: 4, core: 2. Of those that a mesh axis runs over, the one named last changes fastest.
Arguments:
- train_inputs: bfloat16 [512, 8192], P(('row', 'col')), may hold values from -6 to 6
- train_grads: bfloat16 [512, 8192], P(('row', 'col')), may hold values from -6 to 6
- query_inputs: bfloat16 [256, 8192], P(('row', 'col')), may hold values from -6 to 6
- query_grads: bfloat16 [256, 8192], P(('row', 'col')), may hold values from -6 to 6
- input_basis: bfloat16 [8192, 8192], P('row', 'col'), may hold values from -0.0625 to 0.0625
- output_basis: bfloat16 [8192, 8192], P('col', 'row'), may hold values from -0.0625 to 0.0625
- eigenvalues: float32 [8192, 8192], P('row', 'col'), may hold values from 0.5 to 5
- query_starts: int32 [16], replicated, may hold values from 0 to 255, as said below
- query_ends: int32 [16], replicated, may hold values from 1 to 256, as said below
Outputs:
- scores: float32 [16, 512], replicated
Inputs may be any that keep to these rules, and one draw needn't show every extreme that they name: Query q covers the query rows query_starts[q] <= r < query_ends[q]: a nonempty span of at most 128 rows that lies inside one aligned block of 128 rows (rows k * 128 to (k + 1) * 128 - 1); spans of different queries may intersect or share a block. `query_ends`: see query_starts.
All inputs are finite; a program needn't handle non-finite values.
Results may differ from a plain program's by a relative error of at most 0.005.
Values may be sent and summed in bfloat16 or wider, within the bound.
A program may use at most 64 MiB of HBM per device.

v0:
```python
import math

import jax
import jax.numpy as jnp
from jax import lax
from jax.sharding import Mesh
from jax.sharding import PartitionSpec as P

D_IN = 8192
D_OUT = 8192
QBLOCK = 128
COL = ("col_0", "col_1", "col_2")
ROW = ("row_0", "row_1")
ROW_COL = ("row_0", "row_1", "col_0", "col_1", "col_2")


damping = 0.1


def laid_out(parts, dim):
    parts = jnp.moveaxis(parts, 0, dim)
    dims = parts.shape
    return parts.reshape(*dims[:dim], dims[dim] * dims[dim + 1], *dims[dim + 2 :])


def gather_together(arrays, axis, dims):
    line = jnp.concatenate([a.reshape(-1) for a in arrays])
    lines, at, gathered = (lax.all_gather(line, axis), 0, [])
    for a, dim in zip(arrays, dims):
        parts = lines[:, at : at + a.size].reshape(-1, *a.shape)
        gathered.append(laid_out(parts, dim))
        at += a.size
    return tuple(gathered)


def by_axis(value, axes):
    for axis in axes:
        value = lax.psum(value, axis)
    return value


def shards(
    train_inputs,
    train_grads,
    query_inputs,
    query_grads,
    input_basis,
    output_basis,
    eigenvalues,
    query_starts,
    query_ends,
):
    grouped = gather_together((train_inputs, query_inputs), COL, (0, 0))
    train_in, query_in = (
        lax.all_to_all(grouped[0], ROW, split_axis=1, concat_axis=0, tiled=True),
        lax.all_to_all(grouped[1], ROW, split_axis=1, concat_axis=0, tiled=True),
    )
    spread = (
        lax.all_to_all(train_grads, COL, split_axis=1, concat_axis=0, tiled=True),
        lax.all_to_all(query_grads, COL, split_axis=1, concat_axis=0, tiled=True),
    )
    train_out, query_out = gather_together((spread[0], spread[1]), ROW, (0, 0))
    train_in_part = jnp.dot(train_in, input_basis, preferred_element_type=jnp.float32)
    query_in_part = jnp.dot(query_in, input_basis, preferred_element_type=jnp.float32)
    train_out_part = jnp.dot(train_out, output_basis, preferred_element_type=jnp.float32)
    query_out_part = jnp.dot(query_out, output_basis, preferred_element_type=jnp.float32)
    in_sums = lax.psum((train_in_part, query_in_part), ROW)
    out_sums = lax.psum((train_out_part, query_out_part), COL)
    train_in_rot = in_sums[0].astype(jnp.bfloat16)
    query_in_rot = in_sums[1].astype(jnp.bfloat16)
    train_grad_rot = out_sums[0].astype(jnp.bfloat16)
    query_grad_rot = out_sums[1].astype(jnp.bfloat16)
    grads_wide = train_grad_rot.astype(jnp.float32)
    denominator = eigenvalues + damping

    def per_query(span):
        span_start, span_end = span
        block_top = span_start // QBLOCK * QBLOCK
        grad_rows = lax.dynamic_slice_in_dim(query_grad_rot, block_top, QBLOCK, 0)
        input_rows = lax.dynamic_slice_in_dim(query_in_rot, block_top, QBLOCK, 0)
        positions = block_top + jnp.arange(QBLOCK, dtype=jnp.int32)
        inside = (positions >= span_start) & (positions < span_end)
        grad_rows = jnp.where(inside[:, None], grad_rows, jnp.zeros((), grad_rows.dtype))
        outer_sum = lax.dot_general(
            grad_rows, input_rows, (((0,), (0,)), ((), ())), preferred_element_type=jnp.float32
        )
        scaled = (outer_sum / denominator).astype(jnp.bfloat16)
        paired = lax.dot_general(
            train_in_rot, scaled, (((1,), (1,)), ((), ())), preferred_element_type=jnp.float32
        )
        return jnp.sum(grads_wide * paired, axis=1)

    partial_scores = lax.map(per_query, (query_starts, query_ends))
    totals = by_axis(partial_scores, ROW_COL)
    return totals * (1.0 / math.sqrt(D_IN * D_OUT * QBLOCK))


def solution(mesh):
    split = Mesh(mesh.devices.reshape(4, 2, 2, 4, 2), ("row_0", "row_1", "col_0", "col_1", "col_2"))
    placed = (
        P(ROW_COL, None),
        P(ROW_COL, None),
        P(ROW_COL, None),
        P(ROW_COL, None),
        P(ROW, COL),
        P(COL, ROW),
        P(ROW, COL),
        P(),
        P(),
    )
    return jax.shard_map(shards, mesh=split, in_specs=placed, out_specs=P(), check_vma=False)
```

profile of v0, /device:TPU:0, one launch (start us, length us, event | category | flops | bytes accessed | tf_op | source)
XLA Modules:
  0.0 457.3 jit_solution(13673715249605043826)
XLA Ops:
  8.9 12.6 %all_to_all.70 = bf16[2,16,512]{2,0,1:T(2,128)(2,1)S(1)} all-to-all(bf16[2,16,512]{2,0,1:T(2,128)(2,1)} %bitcast.54), channel_id=1, replica_groups=mesh['row_0'=4,'row_1'=2,'col_0'=2,'col_1'=4,'col_2'=2] {'col_0','col_1'..., dimensions={1} | all-to-all | bytes 65536 | tf_op jit(solution)/shard_map/all_to_all | solution.py:60
  21.5 3.5 all-to-all-start
  25.0 3.2 broadcast_add_fusion
  28.3 3.2 all-to-all-done
  31.5 36.2 %all-gather = bf16[393216]{0:T(1024)(128)(2,1)S(1)} all-gather(bf16[49152]{0:T(1024)(128)(2,1)S(1)} %pad_maximum_fusion), channel_id=2, replica_groups=mesh['row_0'=4,'row_1'=2,'col_0'=2,'col_1'=4,'col_2'=2] {'row_0','row_1'}, dimensions={0}, use_global_device_ids=true | all-gather | bytes 884736 | tf_op jit(solution)/shard_map/all_gather | solution.py:28
  69.1 1.8 reshape.40
  71.8 1.3 all_to_all.58
  74.2 5.8 %all-to-all-start.2 = ((bf16[32,8,1024]{2,0,1:T(8,128)(2,1)}), bf16[32,8,1024]{2,0,1:T(8,128)(2,1)}, u32[]{:S(2)}, u32[]{:S(2)}) async-start(bf16[32,8,1024]{2,0,1:T(8,128)(2,1)} %copy.21), calls=%async_computation.2 | async-start | bytes 1048576 | tf_op jit(solution)/shard_map/all_to_all | solution.py:56
  80.0 1.8 fusion.18
  82.6 2.5 fusion.15
  86.1 2.3 all_to_all.62
  88.5 2.8 copy.22
  91.2 7.2 %all-to-all-start.3 = ((bf16[64,8,1024]{2,0,1:T(8,128)(2,1)}), bf16[64,8,1024]{2,0,1:T(8,128)(2,1)}, u32[]{:S(2)}, u32[]{:S(2)}) async-start(bf16[64,8,1024]{2,0,1:T(8,128)(2,1)} %copy.22), calls=%async_computation.3 | async-start | bytes 2097152 | tf_op jit(solution)/shard_map/all_to_all | solution.py:55
  98.4 71.6 %all-reduce.4 = (bf16[256,1024]{1,0:T(8,128)(2,1)}, bf16[512,1024]{1,0:T(8,128)(2,1)}) all-reduce(f32[256,1024]{1,0:T(8,128)} %fusion.15, f32[512,1024]{1,0:T(8,128)S(1)} %fusion.18), channel_id=1, replica_groups=mesh['row_0'=4,'row_1'=2,'col_0'=2,'col_1'=4,'col_2'=2] {'col_0','col_1'..., use_global_device_ids=true, to_apply=%region_0.0 | all-reduce | flops 786432 | bytes 4718592 | tf_op jit(solution)/shard_map/psum | solution.py:68
  170.1 1.5 copy.23
  171.6 2.6 fusion.16
  174.2 3.3 fusion.17
  177.4 91.7 %all-reduce.5 = (bf16[256,512]{1,0:T(8,128)(2,1)}, bf16[512,512]{1,0:T(8,128)(2,1)}) all-reduce(f32[256,512]{1,0:T(8,128)} %fusion.16, f32[512,512]{1,0:T(8,128)} %fusion.17), channel_id=1, replica_groups=mesh['row_0'=4,'row_1'=2,'col_0'=2,'col_1'=4,'col_2'=2] {'row_0','row_1'}, use_global_device_ids=true, to_apply=%region_1.0 | all-reduce | flops 393216 | bytes 2359296 | tf_op jit(solution)/shard_map/psum | solution.py:67
  269.2 127.2 %while.12 = (s32[]{:T(128)}, f32[16,512]{1,0:T(8,128)S(1)}, s32[16]{0:T(128)S(1)}, s32[16]{0:T(128)S(1)}, bf16[256,1024]{1,0:T(8,128)(2,1)}, /*index=5*/bf16[256...) while((s32[]{:T(128)}, f32[16,512]{1,0:T(8,128)S(1)}, ...), condition=%wide.region_6.7_spmd, body=%wide.region_4.6_spmd.sunk | while | flops 673316864 | bytes 5119617 | solution.py:93
  272.9 1.2 compare_and_fusion.2
  274.1 2.9 fusion.35
  280.8 1.2 compare_and_fusion.2
  282.1 2.9 fusion.35
  288.8 1.2 compare_and_fusion.2
  290.0 2.9 fusion.35
  296.7 1.2 compare_and_fusion.2
  298.0 2.9 fusion.35
  304.7 1.2 compare_and_fusion.2
  305.9 2.9 fusion.35
  312.6 1.2 compare_and_fusion.2
  313.9 2.9 fusion.35
  320.6 1.2 compare_and_fusion.2
  321.8 2.9 fusion.35
  328.5 1.2 compare_and_fusion.2
  329.8 2.9 fusion.35
  337.7 2.9 fusion.35
  345.7 2.9 fusion.35
  353.6 2.9 fusion.35
  361.6 2.9 fusion.35
  369.5 2.9 fusion.35
  377.5 2.9 fusion.35
  385.5 2.9 fusion.35
  393.4 2.9 fusion.35
  396.4 15.9 %psum.67 = f32[16,512]{1,0:T(8,128)S(1)} all-reduce(f32[16,512]{1,0:T(8,128)S(1)} %get-tuple-element.119), channel_id=1, replica_groups=mesh['row_0'=4,'row_1'=2,'col_0'=2,'col_1'=4,'col_2'=2] {'row_0'}, use_global_device_ids=true, to_apply=%region_7.8 | all-reduce | flops 8192 | bytes 65536 | tf_op jit(solution)/shard_map/psum | solution.py:38
  412.3 11.0 %psum.68 = f32[16,512]{1,0:T(8,128)S(1)} all-reduce(f32[16,512]{1,0:T(8,128)S(1)} %psum.67), channel_id=1, replica_groups=mesh['row_0'=4,'row_1'=2,'col_0'=2,'col_1'=4,'col_2'=2] {'row_1'}, use_global_device_ids=true, to_apply=%region_8.9 | all-reduce | flops 8192 | bytes 65536 | tf_op jit(solution)/shard_map/psum | solution.py:38
  423.3 8.7 %psum.69 = f32[16,512]{1,0:T(8,128)S(1)} all-reduce(f32[16,512]{1,0:T(8,128)S(1)} %psum.68), channel_id=1, replica_groups=mesh['row_0'=4,'row_1'=2,'col_0'=2,'col_1'=4,'col_2'=2] {'col_0'}, use_global_device_ids=true, to_apply=%region_9.10 | all-reduce | flops 8192 | bytes 65536 | tf_op jit(solution)/shard_map/psum | solution.py:38
  432.0 14.4 %psum.70 = f32[16,512]{1,0:T(8,128)S(1)} all-reduce(f32[16,512]{1,0:T(8,128)S(1)} %psum.69), channel_id=1, replica_groups=mesh['row_0'=4,'row_1'=2,'col_0'=2,'col_1'=4,'col_2'=2] {'col_1'}, use_global_device_ids=true, to_apply=%region_10.11 | all-reduce | flops 8192 | bytes 65536 | tf_op jit(solution)/shard_map/psum | solution.py:38
  446.5 3.4 psum.71
  (90 shorter events, 38.6 us)
Async XLA Ops:
  6.5 73.5 %copy-start = (bf16[512,1024]{1,0:T(8,128)(2,1)S(1)}, bf16[512,1024]{1,0:T(8,128)(2,1)}, u32[]{:S(2)}) copy-start(bf16[512,1024]{1,0:T(8,128)(2,1)} %param.16) | copy-start | bytes 3145732
  6.5 62.5 %all-gather.4.cloned.1.call-start = ((), (), s32[]{:S(2)}) async-start(), calls=%async_computation.4 | async-start | bytes 1671168 | tf_op jit(solution)/shard_map/all_gather | solution.py:28
  21.5 9.9 %all-to-all-start = ((bf16[4,16,512]{2,0,1:T(4,128)(2,1)}), bf16[4,16,512]{2,0,1:T(4,128)(2,1)S(1)}, u32[]{:S(2)}, u32[]{:S(2)}) async-start(bf16[4,16,512]{2,0,1:T(4,128)(2,1)} %bitcast.51), calls=%async_computation | async-start | bytes 131072 | tf_op jit(solution)/shard_map/all_to_all | solution.py:59
  68.0 1.1 copy-start.3
  70.9 3.3 copy-start.1
  74.2 7.5 %slice-start = ((bf16[8,49152]{1,0:T(8,128)(2,1)}), bf16[8,16384]{1,0:T(8,128)(2,1)S(1)}, s32[]{:S(2)}) async-start(bf16[8,49152]{1,0:T(8,128)(2,1)} %copy-done.3), calls=%async_computation.5 | async-start | bytes 524288 | tf_op jit(solution)/shard_map/slice | solution.py:30
  74.2 17.0 %all-to-all-start.2 = ((bf16[32,8,1024]{2,0,1:T(8,128)(2,1)}), bf16[32,8,1024]{2,0,1:T(8,128)(2,1)}, u32[]{:S(2)}, u32[]{:S(2)}) async-start(bf16[32,8,1024]{2,0,1:T(8,128)(2,1)} %copy.21), calls=%async_computation.2 | async-start | bytes 1048576 | tf_op jit(solution)/shard_map/all_to_all | solution.py:56
  82.6 2.5 copy-start.2
  91.2 82.9 %all-to-all-start.3 = ((bf16[64,8,1024]{2,0,1:T(8,128)(2,1)}), bf16[64,8,1024]{2,0,1:T(8,128)(2,1)}, u32[]{:S(2)}, u32[]{:S(2)}) async-start(bf16[64,8,1024]{2,0,1:T(8,128)(2,1)} %copy.22), calls=%async_computation.3 | async-start | bytes 2097152 | tf_op jit(solution)/shard_map/all_to_all | solution.py:55
  174.2 95.0 %copy-start.4 = (s32[16]{0:T(128)S(1)}, s32[16]{0:T(128)}, u32[]{:S(2)}) copy-start(s32[16]{0:T(128)} %param.18) | copy-start | bytes 196
  174.2 95.0 %copy-start.5 = (s32[16]{0:T(128)S(1)}, s32[16]{0:T(128)}, u32[]{:S(2)}) copy-start(s32[16]{0:T(128)} %param.19) | copy-start | bytes 196
Sparse Core Ops, SparseCore 0:
  9.1 37.2 all-gather.3
where the time goes:
time: 461 us; the launch traced here: 457 us
  blocking collectives  266 us (58%)
  matrix products  56.8 us (12%)
  loops' own time  40.5 us (9%)
  local copies, waits for them, and re-layouts  37.2 us (8%)
  other arithmetic  24.1 us (5%)
  starting transfers between devices  16.5 us (4%)
  between operations  13.5 us (3%)
    psum x1, blocking collectives, shards(): in_sums = lax.psum((train_in_part, query_in_part), ROW)  91.7 us
    psum x1, blocking collectives, shards(): out_sums = lax.psum((train_out_part, query_out_part), COL)  71.6 us
    psum x5, blocking collectives, by_axis(): value = lax.psum(value, axis)  53.4 us
    dot_general x16, matrix products, per_query(): lax.dot_general(train_in_rot, scaled, (((1,), (1,)), ((), ())), preferred...  46.7 us
    another operation x1, loops' own time, shards(): partial_scores = lax.map(per_query, (query_starts, query_ends))  40.5 us
    all_gather x1, blocking collectives, gather_together(): lines, at, gathered = (lax.all_gather(line, axis), 0, [])  36.2 us
    and x16, other arithmetic, per_query(): inside = (positions >= span_start) & (positions < span_end)  19.6 us
    dynamic_slice x32, local copies, waits for them, and re-layouts, shards(): partial_scores = lax.map(per_query, (query_starts, query_ends))  19.4 us
  transfers between devices with their start and end apart: 4, of which 1 were waited for; matrix products, arithmetic and copies ran while one was open for 4% of the time, Pallas kernels for 0%

commit v1 on v0

v1 whole, which is shorter than its diff:
```python
import functools
import math

import jax
import jax.numpy as jnp
from jax import lax
from jax.experimental import pallas as pl
from jax.experimental.pallas import tpu as pltpu
from jax.sharding import Mesh
from jax.sharding import PartitionSpec as P

D_IN = 8192
D_OUT = 8192
QBLOCK = 128
NQ = 16
MESH = pl.DeviceIdType.MESH
ROW = ("x", "u")
COL = ("v", "z", "k")
ALL = ("x", "u", "v", "z", "k")
damping = 0.1
BF = jnp.bfloat16
F32 = jnp.float32


def send(src, dst, send_sem, recv_sem, device):
    copy = pltpu.make_async_remote_copy(
        src_ref=src,
        dst_ref=dst,
        send_sem=send_sem,
        recv_sem=recv_sem,
        device_id=device,
        device_id_type=MESH,
    )
    copy.start()
    return copy


def one_hot(rows, cols, source):
    row = lax.broadcasted_iota(jnp.int32, (rows, cols), 0)
    col = lax.broadcasted_iota(jnp.int32, (rows, cols), 1)
    return jnp.where(col == source(row), 1.0, 0.0).astype(BF)


def compact_source(row):
    train = row // 4 * 8 + row % 4
    query = (row - 32) // 2 * 8 + 4 + (row - 32) % 2
    return jnp.where(row < 32, train, query)


def ordered_source(row, outer_is_r):
    train = row < 256
    rest = jnp.where(train, row, row - 256)
    width = jnp.where(train, 4, 2)
    pair = jnp.where(train, rest // 4, rest // 2)
    j = jnp.where(train, rest % 4, rest % 2)
    r, p = pair // 8, pair % 8
    chunk, inner = (r, p) if outer_is_r else (p, r)
    return chunk * 48 + jnp.where(train, 0, 32) + inner * width + j


def rotate_kernel(
    xi, gi, bi, bo, fi, fg,
    ra, rb, ai, ag, bsib, pi, pg, si, sg, ri, rg, ui, ug, hi, hg,
    ssem, rsem,
):
    x, u, v, z, k = (lax.axis_index(a) for a in ALL)
    r, p = x * 2 + u, v * 4 + z
    other = 1 - k

    def row_peer(d):
        q = lax.rem(r + d, 8)
        return q, {"x": q // 2, "u": lax.rem(q, 2)}

    def col_peer(d):
        q = lax.rem(p + d, 8)
        return q, {"v": q // 4, "z": lax.rem(q, 4)}

    barrier = pltpu.get_barrier_semaphore()
    for d in range(1, 8):
        for peer in (row_peer(d)[1], col_peer(d)[1]):
            pl.semaphore_signal(barrier, inc=1, device_id=peer, device_id_type=MESH)
    pl.semaphore_signal(barrier, inc=1, device_id={"k": other}, device_id_type=MESH)
    pl.semaphore_wait(barrier, 15)

    basis_copy = send(
        bo.at[:, pl.ds(pl.multiple_of(other * 512, 512), 512)], bsib,
        ssem.at[0, 0], rsem.at[0, 0], {"k": other},
    )
    first = []
    for d in range(1, 8):
        q, peer = row_peer(d)
        first.append(send(
            xi.at[:, pl.ds(pl.multiple_of(q * 1024, 1024), 1024)], ra.at[r],
            ssem.at[1, d], rsem.at[1, d], peer,
        ))
        q, peer = col_peer(d)
        first.append(send(
            gi.at[:, pl.ds(pl.multiple_of(q * 1024, 1024), 1024)], rb.at[p],
            ssem.at[2, d], rsem.at[2, d], peer,
        ))
    ra[r] = xi[:, pl.ds(pl.multiple_of(r * 1024, 1024), 1024)]
    rb[p] = gi[:, pl.ds(pl.multiple_of(p * 1024, 1024), 1024)]
    pick = one_hot(48, 64, compact_source)
    for copy in first:
        copy.wait()

    ai[k, p] = jnp.dot(pick, ra[...].reshape(64, 1024), preferred_element_type=F32).astype(BF)
    ag[k, r] = jnp.dot(pick, rb[...].reshape(64, 1024), preferred_element_type=F32).astype(BF)
    second = []
    for d in range(1, 8):
        second.append(send(
            ai.at[k, p], ai.at[k, p], ssem.at[3, d], rsem.at[3, d], col_peer(d)[1]
        ))
        second.append(send(
            ag.at[k, r], ag.at[k, r], ssem.at[4, d], rsem.at[4, d], row_peer(d)[1]
        ))
    for copy in second:
        copy.wait()
    swap = [
        send(ai.at[k], ai.at[k], ssem.at[5, 0], rsem.at[5, 0], {"k": other}),
        send(ag.at[k], ag.at[k], ssem.at[5, 1], rsem.at[5, 1], {"k": other}),
    ]
    basis_copy.wait()
    for copy in swap:
        copy.wait()

    own = pl.ds(pl.multiple_of(k * 512, 512), 512)
    far = pl.ds(pl.multiple_of(other * 512, 512), 512)
    for half in range(2):
        rows = pl.ds(half * 384, 384)
        part = jnp.dot(ai[half].reshape(384, 1024), bi[...], preferred_element_type=F32)
        for b in range(4):
            pi[b, rows] = part[:, b * 128 : (b + 1) * 128]
            si[b, rows] = part[:, b * 128 : (b + 1) * 128].astype(BF)
        block = ag.at[half]
        part = jnp.dot(
            block[:, :, own].reshape(384, 512), bo[:, own], preferred_element_type=F32
        ) + jnp.dot(block[:, :, far].reshape(384, 512), bsib[...], preferred_element_type=F32)
        for b in range(4):
            pg[b, rows] = part[:, b * 128 : (b + 1) * 128]
            sg[b, rows] = part[:, b * 128 : (b + 1) * 128].astype(BF)

    third = []
    for d in range(1, 4):
        q = lax.rem(x + d, 4)
        third.append(send(si.at[q], ri.at[d - 1], ssem.at[6, d], rsem.at[6, d], {"x": q}))
        q = lax.rem(z + d, 4)
        third.append(send(sg.at[q], rg.at[d - 1], ssem.at[7, d], rsem.at[7, d], {"z": q}))
    for copy in third:
        copy.wait()

    def total(part, got, place):
        value = part[place]
        for d in range(3):
            value = value + got[d].astype(F32)
        return value

    pi[x] = total(pi, ri, x)
    pg[z] = total(pg, rg, z)

    def half_of(part, place, which):
        return part.at[place, pl.ds(pl.multiple_of(which * 384, 384), 384)]

    fourth = [
        send(half_of(pi, x, 1 - u), ui, ssem.at[8, 0], rsem.at[8, 0], {"u": 1 - u}),
        send(half_of(pg, z, 1 - v), ug, ssem.at[8, 1], rsem.at[8, 1], {"v": 1 - v}),
    ]
    order_in = one_hot(384, 384, functools.partial(ordered_source, outer_is_r=False))
    order_out = one_hot(384, 384, functools.partial(ordered_source, outer_is_r=True))
    for copy in fourth:
        copy.wait()
    done_in = (half_of(pi, x, u)[...] + ui[...]).astype(BF)
    done_out = (half_of(pg, z, v)[...] + ug[...]).astype(BF)
    hi[x, u] = jnp.dot(order_in, done_in, preferred_element_type=F32).astype(BF)
    hg[k, z, v] = jnp.dot(order_out, done_out, preferred_element_type=F32).astype(BF)

    fifth = [
        send(hi.at[x, u], hi.at[x, u], ssem.at[9, 0], rsem.at[9, 0], {"u": 1 - u}),
        send(hg.at[k, z, v], hg.at[k, z, v], ssem.at[9, 1], rsem.at[9, 1], {"v": 1 - v}),
    ]
    for copy in fifth:
        copy.wait()
    sixth = []
    for d in range(1, 4):
        sixth.append(send(
            hi.at[x], hi.at[x], ssem.at[10, d], rsem.at[10, d], {"x": lax.rem(x + d, 4)}
        ))
        sixth.append(send(
            hg.at[k, z], hg.at[k, z], ssem.at[11, d], rsem.at[11, d], {"z": lax.rem(z + d, 4)}
        ))
    for copy in sixth:
        copy.wait()
    last = send(hg.at[k], hg.at[k], ssem.at[12, 0], rsem.at[12, 0], {"k": other})
    fi[...] = hi[...]
    last.wait()
    fg[...] = hg[...]


def rotate(xi, gi, bi, bo):
    vmem = pl.BlockSpec(memory_space=pltpu.VMEM)
    return pl.pallas_call(
        rotate_kernel,
        out_shape=(
            jax.ShapeDtypeStruct((4, 2, 384, 128), BF),
            jax.ShapeDtypeStruct((2, 4, 2, 384, 128), BF),
        ),
        in_specs=[vmem] * 4,
        out_specs=(vmem, vmem),
        scratch_shapes=[
            pltpu.VMEM((8, 8, 1024), BF),
            pltpu.VMEM((8, 8, 1024), BF),
            pltpu.VMEM((2, 8, 48, 1024), BF),
            pltpu.VMEM((2, 8, 48, 1024), BF),
            pltpu.VMEM((512, 512), BF),
            pltpu.VMEM((4, 768, 128), F32),
            pltpu.VMEM((4, 768, 128), F32),
            pltpu.VMEM((4, 768, 128), BF),
            pltpu.VMEM((4, 768, 128), BF),
            pltpu.VMEM((3, 768, 128), BF),
            pltpu.VMEM((3, 768, 128), BF),
            pltpu.VMEM((384, 128), F32),
            pltpu.VMEM((384, 128), F32),
            pltpu.VMEM((4, 2, 384, 128), BF),
            pltpu.VMEM((2, 4, 2, 384, 128), BF),
            pltpu.SemaphoreType.DMA((13, 8)),
            pltpu.SemaphoreType.DMA((13, 8)),
        ],
        compiler_params=pltpu.CompilerParams(
            collective_id=0, has_side_effects=True, vmem_limit_bytes=56 * 2**20
        ),
    )(xi, gi, bi, bo)


def score_kernel(starts, ends, fi, fg, eig, out, inverse, a_query, g_query, a_train, g_train, scaled, acc, stage, ssem, rsem):
    x, u, v, z, k = (lax.axis_index(a) for a in ALL)
    y = u * 2 + v

    def y_peer(d):
        q = lax.rem(y + d, 4)
        return {"u": q // 2, "v": lax.rem(q, 2)}

    def x_peer(d):
        return {"x": lax.rem(x + d, 4)}

    def z_peer(d):
        return {"z": lax.rem(z + d, 4)}

    barrier = pltpu.get_barrier_semaphore()
    for d in range(1, 4):
        for peer in (x_peer(d), y_peer(d), z_peer(d)):
            pl.semaphore_signal(barrier, inc=1, device_id=peer, device_id_type=MESH)
    pl.semaphore_signal(barrier, inc=1, device_id={"k": 1 - k}, device_id_type=MESH)

    inverse[...] = 1.0 / (eig[...] + damping)
    for h in range(2):
        for b in range(4):
            lanes = pl.ds(b * 128, 128)
            a_train[pl.ds(h * 256, 256), lanes] = fi[b, h, 0:256].astype(F32)
            a_query[pl.ds(h * 128, 128), lanes] = fi[b, h, 256:384].astype(F32)
            for s in range(2):
                at = s * 512 + b * 128
                g_train[pl.ds(h * 256, 256), pl.ds(at, 128)] = fg[s, b, h, 0:256]
                turned = jnp.transpose(fg[s, b, h, 256:384].astype(F32), (1, 0))
                g_query[pl.ds(at, 128), pl.ds(h * 128, 128)] = turned.astype(BF)
    acc[...] = jnp.zeros_like(acc)

    def query(q, carry):
        row = lax.broadcasted_iota(jnp.int32, (256, 512), 0)
        h, m = row // 128, row % 128
        true_row = 2 * (16 * (m // 16) + 2 * (m % 16 // 2) + h) + m % 2
        inside = (true_row >= starts[q]) & (true_row < ends[q])
        rows = jnp.where(inside, a_query[...], 0.0).astype(BF)
        for o in range(4):
            at = pl.ds(o * 256, 256)
            outer = jnp.dot(g_query[at, :], rows, preferred_element_type=F32)
            scaled[at, :] = (outer * inverse[at, :]).astype(BF)
        for t in range(2):
            at = pl.ds(t * 256, 256)
            paired = jnp.dot(g_train[at, :], scaled[...], preferred_element_type=F32)
            product = paired * a_train[at, :]
            column = jnp.sum(product, axis=1, keepdims=True)
            lane = lax.broadcasted_iota(jnp.int32, (256, 128), 1)
            acc[at, :] = jnp.where(lane == q, column, acc[at, :])
        return carry

    lax.fori_loop(0, NQ, query, 0)
    value = jnp.transpose(acc[...], (1, 0))[0:NQ]
    pl.semaphore_wait(barrier, 10)

    stage[0, k] = value
    copy = send(stage.at[0, k], stage.at[0, k], ssem.at[0, 0], rsem.at[0, 0], {"k": 1 - k})
    copy.wait()
    value = stage[0, 0] + stage[0, 1]
    for i, (place, peer) in enumerate(((z, z_peer), (x, x_peer), (y, y_peer))):
        n = i + 1
        stage[n, place] = value
        copies = [
            send(stage.at[n, place], stage.at[n, place], ssem.at[n, d], rsem.at[n, d], peer(d))
            for d in range(1, 4)
        ]
        for copy in copies:
            copy.wait()
        value = (stage[n, 0] + stage[n, 1]) + (stage[n, 2] + stage[n, 3])
    out[...] = value


def score(starts, ends, fi, fg, eig):
    vmem = pl.BlockSpec(memory_space=pltpu.VMEM)
    smem = pl.BlockSpec(memory_space=pltpu.SMEM)
    return pl.pallas_call(
        score_kernel,
        out_shape=jax.ShapeDtypeStruct((NQ, 512), F32),
        in_specs=[smem, smem, vmem, vmem, vmem],
        out_specs=vmem,
        scratch_shapes=[
            pltpu.VMEM((1024, 512), F32),
            pltpu.VMEM((256, 512), F32),
            pltpu.VMEM((1024, 256), BF),
            pltpu.VMEM((512, 512), F32),
            pltpu.VMEM((512, 1024), BF),
            pltpu.VMEM((1024, 512), BF),
            pltpu.VMEM((512, 128), F32),
            pltpu.VMEM((4, 4, NQ, 512), F32),
            pltpu.SemaphoreType.DMA((4, 4)),
            pltpu.SemaphoreType.DMA((4, 4)),
        ],
        compiler_params=pltpu.CompilerParams(
            collective_id=1, has_side_effects=True, vmem_limit_bytes=56 * 2**20
        ),
    )(starts, ends, fi, fg, eig)


def shards(
    train_inputs,
    train_grads,
    query_inputs,
    query_grads,
    input_basis,
    output_basis,
    eigenvalues,
    query_starts,
    query_ends,
):
    xi = jnp.pad(jnp.concatenate([train_inputs, query_inputs], 0), ((0, 2), (0, 0)))
    gi = jnp.pad(jnp.concatenate([train_grads, query_grads], 0), ((0, 2), (0, 0)))
    fi, fg = rotate(xi, gi, input_basis, output_basis)
    totals = score(query_starts, query_ends, fi, fg, eigenvalues)
    totals = totals.reshape(NQ, 2, 64, 4).transpose(0, 2, 1, 3).reshape(NQ, 512)
    return totals * (1.0 / math.sqrt(D_IN * D_OUT * QBLOCK))


def solution(mesh):
    split = Mesh(mesh.devices.reshape(4, 2, 2, 4, 2), ALL)
    placed = (
        P(ROW + COL, None),
        P(ROW + COL, None),
        P(ROW + COL, None),
        P(ROW + COL, None),
        P(ROW, COL),
        P(COL, ROW),
        P(ROW, COL),
        P(),
        P(),
    )
    return jax.shard_map(shards, mesh=split, in_specs=placed, out_specs=P(), check_vma=False)
```

time: 461 us -> 119 us (0.26)
  blocking collectives: 266 us -> 0 us
  Pallas kernels: 0 us -> 116 us
  matrix products: 56.8 us -> 0 us
  loops' own time: 40.5 us -> 0 us
  local copies, waits for them, and re-layouts: 37.2 us -> 0.89 us
  other arithmetic: 24.1 us -> 2.55 us
  starting transfers between devices: 16.5 us -> 0 us
  between operations: 13.5 us -> 0.03 us
    psum x7 -> x0, blocking collectives: 217 us -> none  [the longest x1 91.7 us: shards(): in_sums = lax.psum((train_in_part, query_in_part), ROW)]
    pallas_call x0 -> x2, Pallas kernels: none -> 116 us  [the longest x1 80.2 us: rotate(): pl.pallas_call(rotate_kernel, out_shape=(jax.ShapeDtypeStruct((4, 2, 384,...]
    dot_general x20 -> x0, matrix products: 56.8 us -> none  [the longest x16 46.7 us: per_query(): lax.dot_general(train_in_rot, scaled, (((1,), (1,)), ((), ())), preferred...]
    another operation x1 -> x0, loops' own time: 40.5 us -> none  [shards(): partial_scores = lax.map(per_query, (query_starts, query_ends))]
    all_gather x1 -> x0, blocking collectives: 36.2 us -> none  [gather_together(): lines, at, gathered = (lax.all_gather(line, axis), 0, [])]
    and x16 -> x0, other arithmetic: 19.6 us -> none  [per_query(): inside = (positions >= span_start) & (positions < span_end)]
    dynamic_slice x32 -> x0, local copies, waits for them, and re-layouts: 19.4 us -> none  [shards(): partial_scores = lax.map(per_query, (query_starts, query_ends))]
    all_to_all x3 -> x0, starting transfers between devices: 16.5 us -> none  [the longest x1 7.2 us: shards(): lax.all_to_all(grouped[0], ROW, split_axis=1, concat_axis=0, tiled=True)]
  transfers between devices with their start and end apart: 4 -> 0, of which waited for: 1 -> 0; matrix products, arithmetic and copies ran while one was open for 4% -> 0% of each run, Pallas kernels for 0% -> 0%
where the time goes in v1:
time: 119 us
  Pallas kernels  116 us (97%)
  other arithmetic  2.55 us (2%)
    pallas_call x1, Pallas kernels, rotate(): pl.pallas_call(rotate_kernel, out_shape=(jax.ShapeDtypeStruct((4, 2, 384,...  80.2 us
    pallas_call x1, Pallas kernels, score(): pl.pallas_call(score_kernel, out_shape=jax.ShapeDtypeStruct((NQ, 512), F3...  35.5 us

profile of v1, /device:TPU:0, one launch (start us, length us, event | category | flops | bytes accessed | tf_op | source)
XLA Modules:
  0.0 119.1 jit_solution(17464251359513327931)
XLA Ops:
  0.0 1.8 %fusion.4 = (bf16[8,8192]{1,0:T(8,128)(2,1)}, bf16[8,8192]{1,0:T(8,128)(2,1)}) fusion(bf16[2,8192]{1,0:T(2,128)(2,1)} %param.11, bf16[4,8192]{1,0:T(4,128)(2,1)} %param.9, bf16[2,8192]{1,0:T(2,128)(2,1)} %param.12, bf16[4,8192]{1,0:T(4,128)(2,1)} %param.10), kind=kLoop, calls=%fused_computation.5 | loop fusion | flops 851968 | bytes 458752 | tf_op jit(solution)/shard_map/concatenate | solution.py:344
  1.8 80.2 %shard_map.91 = (bf16[4,2,384,128]{3,2,1,0:T(8,128)(2,1)}, bf16[2,4,2,384,128]{4,3,2,1,0:T(8,128)(2,1)}) custom-call(bf16[8,8192]{1,0:T(8,128)(2,1)} %get-tuple-element.9.xi, bf16[8,8192]{1,0:T(8,128)(2,1)} %get-tuple-element.10.gi, bf16[1024,512]{1,0:T(8,128)(2,1)} %bi.1, bf16[512,1024]{1,0:T(8,128)(2,1)} %bo.1), custom_call_target="tpu_custom_call" | custom-call | tf_op jit(solution)/shard_map/pallas_call | solution.py:201
  82.0 35.5 %shard_map.92 = f32[16,512]{1,0:T(8,128)} custom-call(s32[16]{0:T(128)} %starts.1, s32[16]{0:T(128)} %ends.1, bf16[4,2,384,128]{3,2,1,0:T(8,128)(2,1)} %get-tuple-element.7.fi, bf16[2,4,2,384,128]{4,3,2,1,0:T(8,128)(2,1)} %get-tuple-element.8.fg, f32[1024,512]{1,0:T(8,128)} %eig.1), custom_call_target="tpu_custom_call" | custom-call | tf_op jit(solution)/shard_map/pallas_call | solution.py:310
  117.4 0.8 broadcast_multiply_fusion
  118.2 0.1 copy.11
  118.4 0.7 copy.13
  (1 shorter events, 0.0 us)

commit v2 on v0

v2 whole, which is shorter than its diff:
```python
import math

import jax
import jax.numpy as jnp
from jax import lax
from jax.experimental import pallas as pl
from jax.experimental.pallas import tpu as pltpu
from jax.sharding import Mesh
from jax.sharding import PartitionSpec as P

D_IN = 8192
D_OUT = 8192
QBLOCK = 128
NQ = 16
MESH = pl.DeviceIdType.MESH
ROW = ("x", "u")
COL = ("v", "z", "k")
ALL = ("x", "u", "v", "z", "k")
damping = 0.1
BF = jnp.bfloat16
F32 = jnp.float32


def send(src, dst, send_sem, recv_sem, device):
    copy = pltpu.make_async_remote_copy(
        src_ref=src,
        dst_ref=dst,
        send_sem=send_sem,
        recv_sem=recv_sem,
        device_id=device,
        device_id_type=MESH,
    )
    copy.start()
    return copy


def one_hot(rows, cols, source):
    row = lax.broadcasted_iota(jnp.int32, (rows, cols), 0)
    col = lax.broadcasted_iota(jnp.int32, (rows, cols), 1)
    return jnp.where(col == source(row), 1.0, 0.0).astype(BF)


def compact_source(row):
    chunk, inner = row // 16, row % 16
    first = jnp.where(chunk == 0, 4, 2 * chunk - 2)
    return inner // 2 * 8 + first + inner % 2


def swapped_source(row):
    outer, inner, j = row // 16, row // 2 % 8, row % 2
    return inner * 16 + outer * 2 + j


def device_of(row):
    k, z, v = row // 128, row // 32 % 4, row // 16 % 2
    x, u = row // 4 % 4, row // 2 % 2
    return 16 * (2 * x + u) + 8 * v + 2 * z + k


def kernel(
    starts, ends, ti, qi, tg, qg, bi, bo, eig, out,
    xi, gi, ra, rb, ai, ag, bfull, pi, pg, si, sg, ri, rg, ui, ug, hi, hg,
    inverse, a_query, g_query, a_train, g_train, scaled, acc, turn, place, stage,
    ssem, rsem,
):
    x, u, v, z, k = (lax.axis_index(a) for a in ALL)
    r, p = x * 2 + u, v * 4 + z
    other = 1 - k
    y = u * 2 + v

    def row_peer(d):
        q = lax.rem(r + d, 8)
        return q, {"x": q // 2, "u": lax.rem(q, 2)}

    def col_peer(d):
        q = lax.rem(p + d, 8)
        return q, {"v": q // 4, "z": lax.rem(q, 4)}

    def x_peer(d):
        return {"x": lax.rem(x + d, 4)}

    def z_peer(d):
        return {"z": lax.rem(z + d, 4)}

    def y_peer(d):
        q = lax.rem(y + d, 4)
        return {"u": q // 2, "v": lax.rem(q, 2)}

    barrier = pltpu.get_barrier_semaphore()
    for d in range(1, 8):
        for peer in (row_peer(d)[1], col_peer(d)[1]):
            pl.semaphore_signal(barrier, inc=1, device_id=peer, device_id_type=MESH)
    pl.semaphore_signal(barrier, inc=1, device_id={"k": other}, device_id_type=MESH)
    pl.semaphore_signal(barrier, inc=1, device_id={"u": 1 - u, "v": 1 - v}, device_id_type=MESH)

    for rows, train, query in ((xi, ti, qi), (gi, tg, qg)):
        rows[...] = jnp.concatenate(
            [train[...].astype(F32), query[...].astype(F32), jnp.zeros((2, D_IN), F32)], axis=0
        ).astype(BF)
    pl.semaphore_wait(barrier, 16)

    first = []
    for d in range(1, 8):
        q, peer = row_peer(d)
        first.append(send(
            xi.at[:, pl.ds(pl.multiple_of(q * 1024, 1024), 1024)], ra.at[r],
            ssem.at[1, d], rsem.at[1, d], peer,
        ))
        q, peer = col_peer(d)
        first.append(send(
            gi.at[:, pl.ds(pl.multiple_of(q * 1024, 1024), 1024)], rb.at[2 * z + v],
            ssem.at[2, d], rsem.at[2, d], peer,
        ))
    basis_copy = send(
        bo.at[:, pl.ds(pl.multiple_of(other * 512, 512), 512)],
        bfull.at[pl.ds(pl.multiple_of(k * 512, 512), 512)],
        ssem.at[0, 0], rsem.at[0, 0], {"k": other},
    )
    ra[r] = xi[:, pl.ds(pl.multiple_of(r * 1024, 1024), 1024)]
    rb[2 * z + v] = gi[:, pl.ds(pl.multiple_of(p * 1024, 1024), 1024)]
    bfull[pl.ds(pl.multiple_of(k * 512, 512), 512), :] = bo[:, pl.ds(pl.multiple_of(k * 512, 512), 512)]
    inverse[...] = 1.0 / (eig[...] + damping)
    turn[...] = one_hot(128, 128, swapped_source)
    pick = one_hot(48, 64, compact_source)
    for copy in first:
        copy.wait()
    rows_in = jnp.dot(pick, ra[...].reshape(64, 1024), preferred_element_type=F32).astype(BF)
    rows_out = jnp.dot(pick, rb[...].reshape(64, 1024), preferred_element_type=F32).astype(BF)

    moving = {}

    def wait(c, step):
        for copy in moving.pop((c, step)):
            copy.wait()

    def sem(c, step, i):
        at = (3 + c * 8 + step, i)
        return ssem.at[at], rsem.at[at]

    def gather_y(c):
        ai[c, k, z, v] = rows_in[16 * c : 16 * c + 16]
        ag[c, k, x, u] = rows_out[16 * c : 16 * c + 16]
        moving[c, 0] = [
            send(ai.at[c, k, z, v], ai.at[c, k, z, v], *sem(c, 0, 0), {"v": 1 - v}),
            send(ag.at[c, k, x, u], ag.at[c, k, x, u], *sem(c, 0, 1), {"u": 1 - u}),
        ]

    def gather_xz(c):
        wait(c, 0)
        moving[c, 1] = []
        for d in range(1, 4):
            moving[c, 1] += [
                send(ai.at[c, k, z], ai.at[c, k, z], *sem(c, 1, d), z_peer(d)),
                send(ag.at[c, k, x], ag.at[c, k, x], *sem(c, 1, d + 3), x_peer(d)),
            ]

    def swap(c):
        wait(c, 1)
        moving[c, 2] = [
            send(ai.at[c, k], ai.at[c, k], *sem(c, 2, 0), {"k": other}),
            send(ag.at[c, k], ag.at[c, k], *sem(c, 2, 1), {"k": other}),
        ]

    def rotate(c):
        wait(c, 2)
        part = jnp.dot(ai[c].reshape(256, 1024), bi[...], preferred_element_type=F32)
        for b in range(4):
            pi[c, b] = part[:, b * 128 : (b + 1) * 128]
            si[c, b] = part[:, b * 128 : (b + 1) * 128].astype(BF)
        for h in range(2):
            lines = jnp.dot(
                turn[...], ag[c, h].reshape(128, 1024), preferred_element_type=F32
            ).astype(BF)
            part = jnp.dot(lines, bfull[...], preferred_element_type=F32)
            for b in range(4):
                pg[c, b, pl.ds(h * 128, 128)] = part[:, b * 128 : (b + 1) * 128]
                sg[c, b, pl.ds(h * 128, 128)] = part[:, b * 128 : (b + 1) * 128].astype(BF)
        moving[c, 3] = []
        for d in range(1, 4):
            q = lax.rem(x + d, 4)
            moving[c, 3].append(send(si.at[c, q], ri.at[c, d - 1], *sem(c, 3, d), {"x": q}))
            q = lax.rem(z + d, 4)
            moving[c, 3].append(send(sg.at[c, q], rg.at[c, d - 1], *sem(c, 3, d + 3), {"z": q}))

    def half_of(part, c, at, which):
        return part.at[c, at, pl.ds(pl.multiple_of(which * 128, 128), 128)]

    def reduce_y(c):
        wait(c, 3)
        for part, got, at in ((pi, ri, x), (pg, rg, z)):
            value = part[c, at]
            for d in range(3):
                value = value + got[c, d].astype(F32)
            part[c, at] = value
        moving[c, 4] = [
            send(half_of(pi, c, x, 1 - u), ui.at[c], *sem(c, 4, 0), {"u": 1 - u}),
            send(half_of(pg, c, z, 1 - v), ug.at[c], *sem(c, 4, 1), {"v": 1 - v}),
        ]

    def spread_y(c):
        wait(c, 4)
        hi[c, x, u] = (half_of(pi, c, x, u)[...] + ui[c]).astype(BF)
        hg[c, k, z, v] = (half_of(pg, c, z, v)[...] + ug[c]).astype(BF)
        moving[c, 5] = [
            send(hi.at[c, x, u], hi.at[c, x, u], *sem(c, 5, 0), {"u": 1 - u}),
            send(hg.at[c, k, z, v], hg.at[c, k, z, v], *sem(c, 5, 1), {"v": 1 - v}),
        ]

    def spread_xz(c):
        wait(c, 5)
        moving[c, 6] = []
        for d in range(1, 4):
            moving[c, 6] += [
                send(hi.at[c, x], hi.at[c, x], *sem(c, 6, d), x_peer(d)),
                send(hg.at[c, k, z], hg.at[c, k, z], *sem(c, 6, d + 3), z_peer(d)),
            ]

    def spread_core(c):
        wait(c, 6)
        moving[c, 7] = [send(hg.at[c, k], hg.at[c, k], *sem(c, 7, 0), {"k": other})]

    def lay_query():
        wait(0, 7)
        for b in range(4):
            a_query[:, pl.ds(b * 128, 128)] = hi[0, b].reshape(256, 128).astype(F32)
            for s in range(2):
                block = hg[0, s, b].reshape(256, 128).astype(F32)
                g_query[pl.ds(s * 512 + b * 128, 128), :] = jnp.transpose(block, (1, 0)).astype(BF)

    def scale(low, high):
        def body(q, carry):
            row = lax.broadcasted_iota(jnp.int32, (256, 512), 0)
            true_row = 2 * device_of(row) + row % 2
            inside = (true_row >= starts[q]) & (true_row < ends[q])
            rows = jnp.where(inside, a_query[...], 0.0).astype(BF)
            for o in range(4):
                at = pl.ds(o * 256, 256)
                outer = jnp.dot(g_query[at, :], rows, preferred_element_type=F32)
                scaled[q, at, :] = (outer * inverse[at, :]).astype(BF)
            return carry

        lax.fori_loop(low, high, body, 0)

    def pair(c):
        wait(c, 7)
        for b in range(4):
            a_train[:, pl.ds(b * 128, 128)] = hi[c, b].reshape(256, 128).astype(F32)
            for s in range(2):
                g_train[:, pl.ds(s * 512 + b * 128, 128)] = hg[c, s, b].reshape(256, 128)
        rows = pl.ds((c - 1) * 256, 256)

        def body(q, carry):
            paired = jnp.dot(g_train[...], scaled[q], preferred_element_type=F32)
            column = jnp.sum(paired * a_train[...], axis=1, keepdims=True)
            lane = lax.broadcasted_iota(jnp.int32, (256, 128), 1)
            acc[rows, :] = jnp.where(lane == q, column, acc[rows, :])
            return carry

        lax.fori_loop(0, NQ, body, 0)

    for c in range(3):
        gather_y(c)
    for c in range(3):
        gather_xz(c)

    def true_train(row):
        device, chunk, j = row // 4, row // 2 % 2, row % 2
        xu, c = device // 16, device % 16
        return chunk * 256 + c % 2 * 128 + c // 2 % 4 * 32 + c // 8 * 16 + xu * 2 + j

    place[...] = one_hot(512, 512, true_train)
    acc[...] = jnp.zeros_like(acc)
    swap(0)
    basis_copy.wait()
    rotate(0)
    swap(1)
    rotate(1)
    reduce_y(0)
    swap(2)
    rotate(2)
    spread_y(0)
    reduce_y(1)
    spread_xz(0)
    spread_y(1)
    reduce_y(2)
    spread_core(0)
    spread_xz(1)
    spread_y(2)
    lay_query()
    scale(0, 5)
    spread_xz(2)
    scale(5, 10)
    spread_core(1)
    scale(10, 16)
    spread_core(2)
    pair(1)
    pair(2)

    value, total = acc[...], 0.0
    for _ in range(3):
        piece = value.astype(BF)
        value = value - piece.astype(F32)
        total = total + jnp.dot(place[...], piece, preferred_element_type=F32)
    value = jnp.transpose(total, (1, 0))[0:NQ]
    stage[0, k] = value
    send(stage.at[0, k], stage.at[0, k], ssem.at[27, 0], rsem.at[27, 0], {"k": other}).wait()
    value = stage[0, 0] + stage[0, 1]
    for n, (at, peer) in enumerate(((z, z_peer), (x, x_peer), (y, y_peer)), 1):
        stage[n, at] = value
        copies = [
            send(stage.at[n, at], stage.at[n, at], ssem.at[27 + n, d], rsem.at[27 + n, d], peer(d))
            for d in range(1, 4)
        ]
        for copy in copies:
            copy.wait()
        value = (stage[n, 0] + stage[n, 1]) + (stage[n, 2] + stage[n, 3])
    out[...] = value * (1.0 / math.sqrt(D_IN * D_OUT * QBLOCK))


def shards(
    train_inputs,
    train_grads,
    query_inputs,
    query_grads,
    input_basis,
    output_basis,
    eigenvalues,
    query_starts,
    query_ends,
):
    vmem = pl.BlockSpec(memory_space=pltpu.VMEM)
    smem = pl.BlockSpec(memory_space=pltpu.SMEM)
    return pl.pallas_call(
        kernel,
        out_shape=jax.ShapeDtypeStruct((NQ, 512), F32),
        in_specs=[smem, smem] + [vmem] * 7,
        out_specs=vmem,
        scratch_shapes=[
            pltpu.VMEM((8, 8192), BF),
            pltpu.VMEM((8, 8192), BF),
            pltpu.VMEM((8, 8, 1024), BF),
            pltpu.VMEM((8, 8, 1024), BF),
            pltpu.VMEM((3, 2, 4, 2, 16, 1024), BF),
            pltpu.VMEM((3, 2, 4, 2, 16, 1024), BF),
            pltpu.VMEM((1024, 512), BF),
            pltpu.VMEM((3, 4, 256, 128), F32),
            pltpu.VMEM((3, 4, 256, 128), F32),
            pltpu.VMEM((3, 4, 256, 128), BF),
            pltpu.VMEM((3, 4, 256, 128), BF),
            pltpu.VMEM((3, 3, 256, 128), BF),
            pltpu.VMEM((3, 3, 256, 128), BF),
            pltpu.VMEM((3, 128, 128), F32),
            pltpu.VMEM((3, 128, 128), F32),
            pltpu.VMEM((3, 4, 2, 128, 128), BF),
            pltpu.VMEM((3, 2, 4, 2, 128, 128), BF),
            pltpu.VMEM((1024, 512), F32),
            pltpu.VMEM((256, 512), F32),
            pltpu.VMEM((1024, 256), BF),
            pltpu.VMEM((256, 512), F32),
            pltpu.VMEM((256, 1024), BF),
            pltpu.VMEM((NQ, 1024, 512), BF),
            pltpu.VMEM((512, 128), F32),
            pltpu.VMEM((128, 128), BF),
            pltpu.VMEM((512, 512), BF),
            pltpu.VMEM((4, 4, NQ, 512), F32),
            pltpu.SemaphoreType.DMA((31, 8)),
            pltpu.SemaphoreType.DMA((31, 8)),
        ],
        compiler_params=pltpu.CompilerParams(
            collective_id=0, has_side_effects=True, vmem_limit_bytes=56 * 2**20
        ),
    )(
        query_starts, query_ends, train_inputs, query_inputs, train_grads, query_grads,
        input_basis, output_basis, eigenvalues,
    )


def solution(mesh):
    split = Mesh(mesh.devices.reshape(4, 2, 2, 4, 2), ALL)
    placed = (
        P(ROW + COL, None),
        P(ROW + COL, None),
        P(ROW + COL, None),
        P(ROW + COL, None),
        P(ROW, COL),
        P(COL, ROW),
        P(ROW, COL),
        P(),
        P(),
    )
    return jax.shard_map(shards, mesh=split, in_specs=placed, out_specs=P(), check_vma=False)
```

time: 461 us -> 95.7 us (0.21)
  blocking collectives: 266 us -> 0 us
  Pallas kernels: 0 us -> 94.1 us
  matrix products: 56.8 us -> 0 us
  loops' own time: 40.5 us -> 0 us
  local copies, waits for them, and re-layouts: 37.2 us -> 1.38 us
  other arithmetic: 24.1 us -> 0 us
  starting transfers between devices: 16.5 us -> 0 us
  between operations: 13.5 us -> 0.01 us
    psum x7 -> x0, blocking collectives: 217 us -> none  [the longest x1 91.7 us: shards(): in_sums = lax.psum((train_in_part, query_in_part), ROW)]
    pallas_call x0 -> x1, Pallas kernels: none -> 94.1 us  [shards(): pl.pallas_call(kernel, out_shape=jax.ShapeDtypeStruct((NQ, 512), F32), in...]
    dot_general x20 -> x0, matrix products: 56.8 us -> none  [the longest x16 46.7 us: per_query(): lax.dot_general(train_in_rot, scaled, (((1,), (1,)), ((), ())), preferred...]
    another operation x1 -> x0, loops' own time: 40.5 us -> none  [shards(): partial_scores = lax.map(per_query, (query_starts, query_ends))]
    all_gather x1 -> x0, blocking collectives: 36.2 us -> none  [gather_together(): lines, at, gathered = (lax.all_gather(line, axis), 0, [])]
    and x16 -> x0, other arithmetic: 19.6 us -> none  [per_query(): inside = (positions >= span_start) & (positions < span_end)]
    dynamic_slice x32 -> x0, local copies, waits for them, and re-layouts: 19.4 us -> none  [shards(): partial_scores = lax.map(per_query, (query_starts, query_ends))]
    all_to_all x3 -> x0, starting transfers between devices: 16.5 us -> none  [the longest x1 7.2 us: shards(): lax.all_to_all(grouped[0], ROW, split_axis=1, concat_axis=0, tiled=True)]
  transfers between devices with their start and end apart: 4 -> 0, of which waited for: 1 -> 0; matrix products, arithmetic and copies ran while one was open for 4% -> 0% of each run, Pallas kernels for 0% -> 0%
where the time goes in v2:
time: 95.7 us; the launch traced here: 95.5 us
  Pallas kernels  94.1 us (98%)
  local copies, waits for them, and re-layouts  1.38 us (1%)
    pallas_call x1, Pallas kernels, shards(): pl.pallas_call(kernel, out_shape=jax.ShapeDtypeStruct((NQ, 512), F32), in...  94.1 us

profile of v2, /device:TPU:0, one launch (start us, length us, event | category | flops | bytes accessed | tf_op | source)
XLA Modules:
  0.0 95.5 jit_solution(16750248702843664755)
XLA Ops:
  0.0 94.1 %shard_map.91 = f32[16,512]{1,0:T(8,128)} custom-call(s32[16]{0:T(128)} %starts.1, s32[16]{0:T(128)} %ends.1, bf16[4,8192]{1,0:T(4,128)(2,1)} %ti.1, bf16[2,8192]{1,0:T(2,128)(2,1)} %qi.1, bf16[4,8192]{1,0:T(4,128)(2,1)} %tg.1, bf16[2,8192]{1,0:T(2,128)(2,1)} %qg.1, bf16[1024,512]{1,0:T(8,128)(2,1)} %bi.1, bf16[512,1024]{1,0:T(8,128)(2,1)} %bo.1, ...), custom_call_target="tpu_custom_call" | custom-call | tf_op jit(solution)/shard_map/pallas_call | solution.py:333
  94.2 1.4 %copy.11 = f32[16,512]{1,0:T(8,128)} copy(f32[16,512]{1,0:T(8,128)} %shard_map.91) | data formatting | bytes 65536

commit v3 on v2

v3 whole, which is shorter than its diff:
```python
import math

import jax
import jax.numpy as jnp
from jax import lax
from jax.experimental import pallas as pl
from jax.experimental.pallas import tpu as pltpu
from jax.sharding import Mesh
from jax.sharding import PartitionSpec as P

D_IN = 8192
D_OUT = 8192
QBLOCK = 128
NQ = 16
MESH = pl.DeviceIdType.MESH
ROW = ("x", "u")
COL = ("v", "z", "k")
ALL = ("x", "u", "v", "z", "k")
damping = 0.1
BF = jnp.bfloat16
F32 = jnp.float32


def send(src, dst, send_sem, recv_sem, device):
    copy = pltpu.make_async_remote_copy(
        src_ref=src,
        dst_ref=dst,
        send_sem=send_sem,
        recv_sem=recv_sem,
        device_id=device,
        device_id_type=MESH,
    )
    copy.start()
    return copy


def one_hot(rows, cols, source):
    row = lax.broadcasted_iota(jnp.int32, (rows, 1), 0)
    col = lax.broadcasted_iota(jnp.int32, (rows, cols), 1)
    return jnp.where(col == source(row), 1.0, 0.0).astype(BF)


def compact_source(row):
    chunk, inner = row // 16, row % 16
    first = jnp.where(chunk == 0, 4, 2 * chunk - 2)
    return inner // 2 * 8 + first + inner % 2


def swapped_source(row):
    outer, inner, j = row // 16, row // 2 % 8, row % 2
    return inner * 16 + outer * 2 + j


def device_of(row):
    k, z, v = row // 128, row // 32 % 4, row // 16 % 2
    x, u = row // 4 % 4, row // 2 % 2
    return 16 * (2 * x + u) + 8 * v + 2 * z + k


def turned(block):
    return jnp.transpose(block.astype(F32), (1, 0))


def kernel(
    starts, ends, ti, qi, tg, qg, bi_hbm, bo_hbm, eig_hbm, out,
    tiv, qiv, tgv, qgv, bi, bo, eig,
    xi, gi, ra, rb, ai, ag, bfull, pi, pg, si, sg, ri, rg, yqi, yqg, yti, ytg, wti, wtg, hi, hg,
    inverse, a_query, g_query, a_train, g_train, scaled, acc, turn, place, true_rows, stage,
    lsem, ssem, rsem,
):
    x, u, v, z, k = (lax.axis_index(a) for a in ALL)
    r, p = x * 2 + u, v * 4 + z
    other = 1 - k
    y = u * 2 + v

    def row_peer(d):
        q = lax.rem(r + d, 8)
        return q, {"x": q // 2, "u": lax.rem(q, 2)}

    def col_peer(d):
        q = lax.rem(p + d, 8)
        return q, {"v": q // 4, "z": lax.rem(q, 4)}

    def x_peer(d):
        return {"x": lax.rem(x + d, 4)}

    def z_peer(d):
        return {"z": lax.rem(z + d, 4)}

    def y_peer(d):
        q = lax.rem(y + d, 4)
        return {"u": q // 2, "v": lax.rem(q, 2)}

    barrier = pltpu.get_barrier_semaphore()
    for d in range(1, 8):
        for peer in (row_peer(d)[1], col_peer(d)[1]):
            pl.semaphore_signal(barrier, inc=1, device_id=peer, device_id_type=MESH)
    pl.semaphore_signal(barrier, inc=1, device_id={"k": other}, device_id_type=MESH)
    pl.semaphore_signal(barrier, inc=1, device_id={"u": 1 - u, "v": 1 - v}, device_id_type=MESH)

    local = []
    for i, (src, dst) in enumerate((
        (ti, tiv), (qi, qiv), (tg, tgv), (qg, qgv), (bo_hbm, bo), (bi_hbm, bi), (eig_hbm, eig)
    )):
        local.append(pltpu.make_async_copy(src, dst, lsem.at[i]))
        local[-1].start()
    for copy in local[:4]:
        copy.wait()
    for rows, train, query in ((xi, tiv, qiv), (gi, tgv, qgv)):
        rows[...] = jnp.concatenate(
            [train[...].astype(F32), query[...].astype(F32), jnp.zeros((2, D_IN), F32)], axis=0
        ).astype(BF)
    pl.semaphore_wait(barrier, 16)

    first = ([], [])
    for d in range(1, 8):
        q, peer = row_peer(d)
        first[0].append(send(
            xi.at[:, pl.ds(pl.multiple_of(q * 1024, 1024), 1024)], ra.at[r],
            ssem.at[1, d], rsem.at[1, d], peer,
        ))
        q, peer = col_peer(d)
        first[1].append(send(
            gi.at[:, pl.ds(pl.multiple_of(q * 1024, 1024), 1024)], rb.at[2 * z + v],
            ssem.at[2, d], rsem.at[2, d], peer,
        ))
    ra[r] = xi[:, pl.ds(pl.multiple_of(r * 1024, 1024), 1024)]
    rb[2 * z + v] = gi[:, pl.ds(pl.multiple_of(p * 1024, 1024), 1024)]
    pick = one_hot(48, 64, compact_source)
    local[4].wait()
    basis_copy = send(
        bo.at[:, pl.ds(pl.multiple_of(other * 512, 512), 512)],
        bfull.at[pl.ds(pl.multiple_of(k * 512, 512), 512)],
        ssem.at[0, 0], rsem.at[0, 0], {"k": other},
    )
    turn[...] = one_hot(128, 128, swapped_source)
    lanes = lax.broadcasted_iota(jnp.int32, (1, 256), 1)
    true_rows[...] = 2 * device_of(lanes) + lanes % 2

    moving = {}

    def wait(*key):
        for copy in moving.pop(key):
            copy.wait()

    def sems(side, c, step, i):
        at = (3 + side * 18 + c * 6 + step, i)
        return ssem.at[at], rsem.at[at]

    gathered = (ai, ag)
    gather_at = ((z, v), (x, u))
    gather_y_peer = ({"v": 1 - v}, {"u": 1 - u})
    gather_peer = (z_peer, x_peer)
    sum_at = (x, z)
    sum_name = ("x", "z")
    sum_y_peer = ({"u": 1 - u}, {"v": 1 - v})
    part = (pi, pg)
    small = (si, sg)
    got = (ri, rg)
    wide_y = (yqi, yqg)
    mine_y = (wti, wtg)
    their_y = (yti, ytg)

    def gather_y(side, rows):
        at = gather_at[side]
        for c in range(3):
            ref = gathered[side].at[c, k, at[0], at[1]]
            ref[...] = rows[16 * c : 16 * c + 16]
            moving[side, c, 0] = [send(ref, ref, *sems(side, c, 0, 0), gather_y_peer[side])]

    def gather_xz(side, c):
        wait(side, c, 0)
        ref = gathered[side].at[c, k, gather_at[side][0]]
        moving[side, c, 1] = [
            send(ref, ref, *sems(side, c, 1, d), gather_peer[side](d)) for d in range(1, 4)
        ]

    def swap(c):
        for side in range(2):
            wait(side, c, 1)
            ref = gathered[side].at[c, k]
            moving[side, c, 2] = [send(ref, ref, *sems(side, c, 2, 0), {"k": other})]

    def rotate(c):
        for side in range(2):
            wait(side, c, 2)
            if side == 0:
                blocks = [(0, 256, ai[c].reshape(256, 1024), bi)]
            else:
                blocks = [
                    (h * 128, 128, jnp.dot(
                        turn[...], ag[c, h].reshape(128, 1024), preferred_element_type=F32
                    ).astype(BF), bfull)
                    for h in range(2)
                ]
            for low, size, rows, basis in blocks:
                value = jnp.dot(rows, basis[...], preferred_element_type=F32)
                for b in range(4):
                    piece = value[:, b * 128 : (b + 1) * 128]
                    part[side][c, b, pl.ds(low, size)] = piece
                    small[side][c, b, pl.ds(low, size)] = piece.astype(BF)
            moving[side, c, 3] = []
            for d in range(1, 4):
                q = lax.rem(sum_at[side] + d, 4)
                moving[side, c, 3].append(send(
                    small[side].at[c, q], got[side].at[c, d - 1], *sems(side, c, 3, d),
                    {sum_name[side]: q},
                ))

    def reduce_y(c):
        for side in range(2):
            wait(side, c, 3)
            at = sum_at[side]
            value = part[side][c, at]
            for d in range(3):
                value = value + got[side][c, d].astype(F32)
            part[side][c, at] = value
            if c == 0:
                src, dst = part[side].at[c, at], wide_y[side]
            else:
                mine_y[side][c - 1] = value.astype(BF)
                src, dst = mine_y[side].at[c - 1], their_y[side].at[c - 1]
            moving[side, c, 4] = [send(src, dst, *sems(side, c, 4, 0), sum_y_peer[side])]

    def spread(c):
        for side in range(2):
            wait(side, c, 4)
            at = sum_at[side]
            more = wide_y[side][...] if c == 0 else their_y[side][c - 1].astype(F32)
            ref = hi.at[c, at] if side == 0 else hg.at[c, k, at]
            ref[...] = (part[side][c, at] + more).astype(BF)
            peer = x_peer if side == 0 else z_peer
            moving[side, c, 5] = [
                send(ref, ref, *sems(side, c, 5, d), peer(d)) for d in range(1, 4)
            ]

    def spread_core(c):
        wait(1, c, 5)
        moving[1, c, 6] = [send(hg.at[c, k], hg.at[c, k], *sems(0, c, 5, 6), {"k": other})]

    def lay_query():
        wait(0, 0, 5)
        for b in range(4):
            a_query[pl.ds(b * 128, 128), :] = turned(hi[0, b])
        wait(1, 0, 6)
        for b in range(4):
            for s in range(2):
                g_query[:, pl.ds(s * 512 + b * 128, 128)] = hg[0, s, b]

    def scale(low, high):
        def body(q, carry):
            inside = (true_rows[...] >= starts[q]) & (true_rows[...] < ends[q])
            rows = jnp.where(inside, a_query[...], 0.0).astype(BF)
            for o in range(4):
                at = pl.ds(o * 256, 256)
                outer = jnp.dot(rows, g_query[:, at], preferred_element_type=F32)
                scaled[q, :, at] = (outer * inverse[:, at]).astype(BF)
            return carry

        lax.fori_loop(low, high, body, 0, unroll=high - low)

    def lay_train(c):
        wait(0, c, 5)
        for b in range(4):
            a_train[c - 1, pl.ds(b * 128, 128), :] = turned(hi[c, b])
        wait(1, c, 6)
        for b in range(4):
            for s in range(2):
                g_train[c - 1, pl.ds(s * 512 + b * 128, 128), :] = turned(hg[c, s, b]).astype(BF)

    def pair(c, low, high):
        def body(q, carry):
            paired = jnp.dot(scaled[q], g_train[c - 1], preferred_element_type=F32)
            acc[c - 1, pl.ds(q, 1), :] = jnp.sum(paired * a_train[c - 1], axis=0, keepdims=True)
            return carry

        lax.fori_loop(low, high, body, 0, unroll=high - low)

    score_at = (k, z, x, y)
    score_peer = (lambda d: {"k": other}, z_peer, x_peer, y_peer)

    def share(half, n):
        if n == 0:
            value = acc[half]
        else:
            value = summed(half, n - 1)
        stage[half, n, score_at[n]] = value
        ref = stage.at[half, n, score_at[n]]
        moving[half, n] = [
            send(ref, ref, ssem.at[39 + half * 4 + n, d], rsem.at[39 + half * 4 + n, d], score_peer[n](d))
            for d in range(1, 2 if n == 0 else 4)
        ]

    def summed(half, n):
        wait(half, n)
        value = stage[half, n, 0] + stage[half, n, 1]
        if n:
            value = value + (stage[half, n, 2] + stage[half, n, 3])
        return value

    def in_order(value, half):
        total = 0.0
        for _ in range(3):
            piece = value.astype(BF)
            value = value - piece.astype(F32)
            total = total + jnp.dot(piece, place[half], preferred_element_type=F32)
        return total

    for side, rows in ((0, ra), (1, rb)):
        for copy in first[side]:
            copy.wait()
        gather_y(side, jnp.dot(pick, rows[...].reshape(64, 1024), preferred_element_type=F32).astype(BF))
    bfull[pl.ds(pl.multiple_of(k * 512, 512), 512), :] = bo[:, pl.ds(pl.multiple_of(k * 512, 512), 512)]
    for c in range(3):
        for side in range(2):
            gather_xz(side, c)

    train = lax.broadcasted_iota(jnp.int32, (1, 512), 1)
    device = train // 4
    spot = train // 2 % 2 * 256 + device % 2 * 128 + device // 2 % 4 * 32 + device % 16 // 8 * 16
    spot = spot + device // 16 * 2 + train % 2
    row = lax.broadcasted_iota(jnp.int32, (512, 512), 0)
    place[...] = jnp.where(row == spot, 1.0, 0.0).astype(BF).reshape(2, 256, 512)
    local[5].wait()
    basis_copy.wait()
    swap(0)
    rotate(0)
    swap(1)
    rotate(1)
    swap(2)
    rotate(2)
    local[6].wait()
    inverse[...] = jnp.transpose(1.0 / (eig[...] + damping), (1, 0))
    reduce_y(0)
    reduce_y(1)
    spread(0)
    reduce_y(2)
    spread(1)
    spread(2)
    spread_core(0)
    lay_query()
    scale(0, 8)
    spread_core(1)
    spread_core(2)
    scale(8, 16)
    lay_train(1)
    pair(1, 0, 16)
    share(0, 0)
    lay_train(2)
    pair(2, 0, 8)
    share(0, 1)
    pair(2, 8, 16)
    share(1, 0)
    share(0, 2)
    share(1, 1)
    share(0, 3)
    share(1, 2)
    early = in_order(summed(0, 3), 0)
    share(1, 3)
    total = early + in_order(summed(1, 3), 1)
    out[...] = total * (1.0 / math.sqrt(D_IN * D_OUT * QBLOCK))


def shards(
    train_inputs,
    train_grads,
    query_inputs,
    query_grads,
    input_basis,
    output_basis,
    eigenvalues,
    query_starts,
    query_ends,
):
    vmem = pl.BlockSpec(memory_space=pltpu.VMEM)
    smem = pl.BlockSpec(memory_space=pltpu.SMEM)
    return pl.pallas_call(
        kernel,
        out_shape=jax.ShapeDtypeStruct((NQ, 512), F32),
        in_specs=[smem, smem] + [pl.BlockSpec(memory_space=pl.ANY)] * 7,
        out_specs=vmem,
        scratch_shapes=[
            pltpu.VMEM((4, 8192), BF),
            pltpu.VMEM((2, 8192), BF),
            pltpu.VMEM((4, 8192), BF),
            pltpu.VMEM((2, 8192), BF),
            pltpu.VMEM((1024, 512), BF),
            pltpu.VMEM((512, 1024), BF),
            pltpu.VMEM((1024, 512), F32),
            pltpu.VMEM((8, 8192), BF),
            pltpu.VMEM((8, 8192), BF),
            pltpu.VMEM((8, 8, 1024), BF),
            pltpu.VMEM((8, 8, 1024), BF),
            pltpu.VMEM((3, 2, 4, 2, 16, 1024), BF),
            pltpu.VMEM((3, 2, 4, 2, 16, 1024), BF),
            pltpu.VMEM((1024, 512), BF),
            pltpu.VMEM((3, 4, 256, 128), F32),
            pltpu.VMEM((3, 4, 256, 128), F32),
            pltpu.VMEM((3, 4, 256, 128), BF),
            pltpu.VMEM((3, 4, 256, 128), BF),
            pltpu.VMEM((3, 3, 256, 128), BF),
            pltpu.VMEM((3, 3, 256, 128), BF),
            pltpu.VMEM((256, 128), F32),
            pltpu.VMEM((256, 128), F32),
            pltpu.VMEM((2, 256, 128), BF),
            pltpu.VMEM((2, 256, 128), BF),
            pltpu.VMEM((2, 256, 128), BF),
            pltpu.VMEM((2, 256, 128), BF),
            pltpu.VMEM((3, 4, 256, 128), BF),
            pltpu.VMEM((3, 2, 4, 256, 128), BF),
            pltpu.VMEM((512, 1024), F32),
            pltpu.VMEM((512, 256), F32),
            pltpu.VMEM((256, 1024), BF),
            pltpu.VMEM((2, 512, 256), F32),
            pltpu.VMEM((2, 1024, 256), BF),
            pltpu.VMEM((NQ, 512, 1024), BF),
            pltpu.VMEM((2, NQ, 256), F32),
            pltpu.VMEM((128, 128), BF),
            pltpu.VMEM((2, 256, 512), BF),
            pltpu.VMEM((1, 256), jnp.int32),
            pltpu.VMEM((2, 4, 4, NQ, 256), F32),
            pltpu.SemaphoreType.DMA((7,)),
            pltpu.SemaphoreType.DMA((47, 8)),
            pltpu.SemaphoreType.DMA((47, 8)),
        ],
        compiler_params=pltpu.CompilerParams(
            collective_id=0, has_side_effects=True, vmem_limit_bytes=56 * 2**20
        ),
    )(
        query_starts, query_ends, train_inputs, query_inputs, train_grads, query_grads,
        input_basis, output_basis, eigenvalues,
    )


def solution(mesh):
    split = Mesh(mesh.devices.reshape(4, 2, 2, 4, 2), ALL)
    placed = (
        P(ROW + COL, None),
        P(ROW + COL, None),
        P(ROW + COL, None),
        P(ROW + COL, None),
        P(ROW, COL),
        P(COL, ROW),
        P(ROW, COL),
        P(),
        P(),
    )
    return jax.shard_map(shards, mesh=split, in_specs=placed, out_specs=P(), check_vma=False)
```

time: 95.7 us -> 85.2 us (0.89)
  Pallas kernels: 94.1 us -> 83.7 us
    pallas_call x1, Pallas kernels: 94.1 us -> 83.7 us  [shards(): pl.pallas_call(kernel, out_shape=jax.ShapeDtypeStruct((NQ, 512), F32), in...]
where the time goes in v3:
time: 85.2 us; the launch traced here: 85.1 us
  Pallas kernels  83.7 us (98%)
  local copies, waits for them, and re-layouts  1.38 us (2%)
    pallas_call x1, Pallas kernels, shards(): pl.pallas_call(kernel, out_shape=jax.ShapeDtypeStruct((NQ, 512), F32), in...  83.7 us

profile of v3, /device:TPU:0, one launch (start us, length us, event | category | flops | bytes accessed | tf_op | source)
XLA Modules:
  0.0 85.1 jit_solution(14269094728275538516)
XLA Ops:
  0.0 83.7 %shard_map.91 = f32[16,512]{1,0:T(8,128)} custom-call(s32[16]{0:T(128)} %starts.1, s32[16]{0:T(128)} %ends.1, bf16[4,8192]{1,0:T(4,128)(2,1)} %ti.1, bf16[2,8192]{1,0:T(2,128)(2,1)} %qi.1, bf16[4,8192]{1,0:T(4,128)(2,1)} %tg.1, bf16[2,8192]{1,0:T(2,128)(2,1)} %qg.1, bf16[1024,512]{1,0:T(8,128)(2,1)} %bi_hbm.1, bf16[512,1024]{1,0:T(8,128)(2,1)} %bo_hbm.1, ...), custom_call_target="tpu_custom_call" | custom-call | tf_op jit(solution)/shard_map/pallas_call | solution.py:377
  83.7 1.4 %copy.11 = f32[16,512]{1,0:T(8,128)} copy(f32[16,512]{1,0:T(8,128)} %shard_map.91) | data formatting | bytes 65536

commit v4 on v3

--- a/solution.py
+++ b/solution.py
@@ -32,6 +32,17 @@
     )
     copy.start()
     return copy
+
+
+def arrival(ref, send_sem, recv_sem, device):
+    return pltpu.make_async_remote_copy(
+        src_ref=ref,
+        dst_ref=ref,
+        send_sem=send_sem,
+        recv_sem=recv_sem,
+        device_id=device,
+        device_id_type=MESH,
+    )
 
 
 def one_hot(rows, cols, source):
@@ -112,18 +123,21 @@
         ).astype(BF)
     pl.semaphore_wait(barrier, 16)
 
-    first = ([], [])
     for d in range(1, 8):
         q, peer = row_peer(d)
-        first[0].append(send(
+        send(
             xi.at[:, pl.ds(pl.multiple_of(q * 1024, 1024), 1024)], ra.at[r],
-            ssem.at[1, d], rsem.at[1, d], peer,
-        ))
+            ssem.at[1], rsem.at[1], peer,
+        )
         q, peer = col_peer(d)
-        first[1].append(send(
+        send(
             gi.at[:, pl.ds(pl.multiple_of(q * 1024, 1024), 1024)], rb.at[2 * z + v],
-            ssem.at[2, d], rsem.at[2, d], peer,
-        ))
+            ssem.at[2], rsem.at[2], peer,
+        )
+    first = (
+        arrival(ra.at[0:7], ssem.at[1], rsem.at[1], row_peer(1)[1]),
+        arrival(rb.at[0:7], ssem.at[2], rsem.at[2], col_peer(1)[1]),
+    )
     ra[r] = xi[:, pl.ds(pl.multiple_of(r * 1024, 1024), 1024)]
     rb[2 * z + v] = gi[:, pl.ds(pl.multiple_of(p * 1024, 1024), 1024)]
     pick = one_hot(48, 64, compact_source)
@@ -131,7 +145,7 @@
     basis_copy = send(
         bo.at[:, pl.ds(pl.multiple_of(other * 512, 512), 512)],
         bfull.at[pl.ds(pl.multiple_of(k * 512, 512), 512)],
-        ssem.at[0, 0], rsem.at[0, 0], {"k": other},
+        ssem.at[0], rsem.at[0], {"k": other},
     )
     turn[...] = one_hot(128, 128, swapped_source)
     lanes = lax.broadcasted_iota(jnp.int32, (1, 256), 1)
@@ -140,12 +154,10 @@
     moving = {}
 
     def wait(*key):
-        for copy in moving.pop(key):
-            copy.wait()
-
-    def sems(side, c, step, i):
-        at = (3 + side * 18 + c * 6 + step, i)
-        return ssem.at[at], rsem.at[at]
+        moving.pop(key).wait()
+
+    def sems(side, c, step):
+        return ssem.at[3 + side * 3 + c], rsem.at[3 + (side * 3 + c) * 7 + step]
 
     gathered = (ai, ag)
     gather_at = ((z, v), (x, u))
@@ -166,20 +178,22 @@
         for c in range(3):
             ref = gathered[side].at[c, k, at[0], at[1]]
             ref[...] = rows[16 * c : 16 * c + 16]
-            moving[side, c, 0] = [send(ref, ref, *sems(side, c, 0, 0), gather_y_peer[side])]
+            moving[side, c, 0] = send(ref, ref, *sems(side, c, 0), gather_y_peer[side])
 
     def gather_xz(side, c):
         wait(side, c, 0)
         ref = gathered[side].at[c, k, gather_at[side][0]]
-        moving[side, c, 1] = [
-            send(ref, ref, *sems(side, c, 1, d), gather_peer[side](d)) for d in range(1, 4)
-        ]
+        for d in range(1, 4):
+            send(ref, ref, *sems(side, c, 1), gather_peer[side](d))
+        moving[side, c, 1] = arrival(
+            gathered[side].at[c, k, 0:3], *sems(side, c, 1), gather_peer[side](1)
+        )
 
     def swap(c):
         for side in range(2):
             wait(side, c, 1)
             ref = gathered[side].at[c, k]
-            moving[side, c, 2] = [send(ref, ref, *sems(side, c, 2, 0), {"k": other})]
+            moving[side, c, 2] = send(ref, ref, *sems(side, c, 2), {"k": other})
 
     def rotate(c):
         for side in range(2):
@@ -199,13 +213,13 @@
                     piece = value[:, b * 128 : (b + 1) * 128]
                     part[side][c, b, pl.ds(low, size)] = piece
                     small[side][c, b, pl.ds(low, size)] = piece.astype(BF)
-            moving[side, c, 3] = []
             for d in range(1, 4):
                 q = lax.rem(sum_at[side] + d, 4)
-                moving[side, c, 3].append(send(
-                    small[side].at[c, q], got[side].at[c, d - 1], *sems(side, c, 3, d),
+                send(
+                    small[side].at[c, q], got[side].at[c, d - 1], *sems(side, c, 3),
                     {sum_name[side]: q},
-                ))
+                )
+            moving[side, c, 3] = arrival(got[side].at[c], *sems(side, c, 3), {sum_name[side]: q})
 
     def reduce_y(c):
         for side in range(2):
@@ -220,7 +234,7 @@
             else:
                 mine_y[side][c - 1] = value.astype(BF)
                 src, dst = mine_y[side].at[c - 1], their_y[side].at[c - 1]
-            moving[side, c, 4] = [send(src, dst, *sems(side, c, 4, 0), sum_y_peer[side])]
+            moving[side, c, 4] = send(src, dst, *sems(side, c, 4), sum_y_peer[side])
 
     def spread(c):
         for side in range(2):
@@ -230,13 +244,14 @@
             ref = hi.at[c, at] if side == 0 else hg.at[c, k, at]
             ref[...] = (part[side][c, at] + more).astype(BF)
             peer = x_peer if side == 0 else z_peer
-            moving[side, c, 5] = [
-                send(ref, ref, *sems(side, c, 5, d), peer(d)) for d in range(1, 4)
-            ]
+            for d in range(1, 4):
+                send(ref, ref, *sems(side, c, 5), peer(d))
+            three = hi.at[c, 0:3] if side == 0 else hg.at[c, k, 0:3]
+            moving[side, c, 5] = arrival(three, *sems(side, c, 5), peer(1))
 
     def spread_core(c):
         wait(1, c, 5)
-        moving[1, c, 6] = [send(hg.at[c, k], hg.at[c, k], *sems(0, c, 5, 6), {"k": other})]
+        moving[1, c, 6] = send(hg.at[c, k], hg.at[c, k], *sems(1, c, 6), {"k": other})
 
     def lay_query():
         wait(0, 0, 5)
@@ -286,10 +301,13 @@
             value = summed(half, n - 1)
         stage[half, n, score_at[n]] = value
         ref = stage.at[half, n, score_at[n]]
-        moving[half, n] = [
-            send(ref, ref, ssem.at[39 + half * 4 + n, d], rsem.at[39 + half * 4 + n, d], score_peer[n](d))
-            for d in range(1, 2 if n == 0 else 4)
-        ]
+        pair_of = (ssem.at[9 + half], rsem.at[45 + half * 4 + n])
+        if n == 0:
+            moving[half, n] = send(ref, ref, *pair_of, score_peer[n](1))
+        else:
+            for d in range(1, 4):
+                send(ref, ref, *pair_of, score_peer[n](d))
+            moving[half, n] = arrival(stage.at[half, n, 0:3], *pair_of, score_peer[n](1))
 
     def summed(half, n):
         wait(half, n)
@@ -307,8 +325,7 @@
         return total
 
     for side, rows in ((0, ra), (1, rb)):
-        for copy in first[side]:
-            copy.wait()
+        first[side].wait()
         gather_y(side, jnp.dot(pick, rows[...].reshape(64, 1024), preferred_element_type=F32).astype(BF))
     bfull[pl.ds(pl.multiple_of(k * 512, 512), 512), :] = bo[:, pl.ds(pl.multiple_of(k * 512, 512), 512)]
     for c in range(3):
@@ -420,8 +437,8 @@
             pltpu.VMEM((1, 256), jnp.int32),
             pltpu.VMEM((2, 4, 4, NQ, 256), F32),
             pltpu.SemaphoreType.DMA((7,)),
-            pltpu.SemaphoreType.DMA((47, 8)),
-            pltpu.SemaphoreType.DMA((47, 8)),
+            pltpu.SemaphoreType.DMA((11,)),
+            pltpu.SemaphoreType.DMA((53,)),
         ],
         compiler_params=pltpu.CompilerParams(
             collective_id=0, has_side_effects=True, vmem_limit_bytes=56 * 2**20

time: 85.2 us -> 79 us (0.927)
  Pallas kernels: 83.7 us -> 77.5 us
    pallas_call x1, Pallas kernels: 83.7 us -> 77.5 us  [shards(): pl.pallas_call(kernel, out_shape=jax.ShapeDtypeStruct((NQ, 512), F32), in...]
where the time goes in v4:
time: 79 us; the launch traced here: 78.8 us
  Pallas kernels  77.5 us (98%)
  local copies, waits for them, and re-layouts  1.38 us (2%)
    pallas_call x1, Pallas kernels, shards(): pl.pallas_call(kernel, out_shape=jax.ShapeDtypeStruct((NQ, 512), F32), in...  77.5 us

profile of v4, /device:TPU:0, one launch (start us, length us, event | category | flops | bytes accessed | tf_op | source)
XLA Modules:
  0.0 78.8 jit_solution(746015843770323440)
XLA Ops:
  0.0 77.5 %shard_map.91 = f32[16,512]{1,0:T(8,128)} custom-call(s32[16]{0:T(128)} %starts.1, s32[16]{0:T(128)} %ends.1, bf16[4,8192]{1,0:T(4,128)(2,1)} %ti.1, bf16[2,8192]{1,0:T(2,128)(2,1)} %qi.1, bf16[4,8192]{1,0:T(4,128)(2,1)} %tg.1, bf16[2,8192]{1,0:T(2,128)(2,1)} %qg.1, bf16[1024,512]{1,0:T(8,128)(2,1)} %bi_hbm.1, bf16[512,1024]{1,0:T(8,128)(2,1)} %bo_hbm.1, ...), custom_call_target="tpu_custom_call" | custom-call | tf_op jit(solution)/shard_map/pallas_call | solution.py:394
  77.5 1.4 %copy.11 = f32[16,512]{1,0:T(8,128)} copy(f32[16,512]{1,0:T(8,128)} %shard_map.91) | data formatting | bytes 65536

commit v5 on v4

--- a/solution.py
+++ b/solution.py
@@ -68,6 +68,12 @@
     return 16 * (2 * x + u) + 8 * v + 2 * z + k
 
 
+def tree(values):
+    while len(values) > 1:
+        values = [a + b for a, b in zip(values[::2], values[1::2])]
+    return values[0]
+
+
 def turned(block):
     return jnp.transpose(block.astype(F32), (1, 0))
 
@@ -76,13 +82,13 @@
     starts, ends, ti, qi, tg, qg, bi_hbm, bo_hbm, eig_hbm, out,
     tiv, qiv, tgv, qgv, bi, bo, eig,
     xi, gi, ra, rb, ai, ag, bfull, pi, pg, si, sg, ri, rg, yqi, yqg, yti, ytg, wti, wtg, hi, hg,
-    inverse, a_query, g_query, a_train, g_train, scaled, acc, turn, place, true_rows, stage,
+    inverse, a_query, g_query, a_train, g_train, scaled, acc, turn, place, true_rows, near_sums, plane_sums,
     lsem, ssem, rsem,
 ):
     x, u, v, z, k = (lax.axis_index(a) for a in ALL)
     r, p = x * 2 + u, v * 4 + z
     other = 1 - k
-    y = u * 2 + v
+    near, plane = u * 4 + v * 2 + k, x * 4 + z
 
     def row_peer(d):
         q = lax.rem(r + d, 8)
@@ -98,16 +104,19 @@
     def z_peer(d):
         return {"z": lax.rem(z + d, 4)}
 
-    def y_peer(d):
-        q = lax.rem(y + d, 4)
-        return {"u": q // 2, "v": lax.rem(q, 2)}
+    def near_peer(d):
+        q = lax.rem(near + d, 8)
+        return {"u": q // 4, "v": lax.rem(q // 2, 2), "k": lax.rem(q, 2)}
+
+    def plane_peer(d):
+        q = lax.rem(plane + d, 16)
+        return {"x": q // 4, "z": lax.rem(q, 4)}
 
     barrier = pltpu.get_barrier_semaphore()
     for d in range(1, 8):
         for peer in (row_peer(d)[1], col_peer(d)[1]):
             pl.semaphore_signal(barrier, inc=1, device_id=peer, device_id_type=MESH)
     pl.semaphore_signal(barrier, inc=1, device_id={"k": other}, device_id_type=MESH)
-    pl.semaphore_signal(barrier, inc=1, device_id={"u": 1 - u, "v": 1 - v}, device_id_type=MESH)
 
     local = []
     for i, (src, dst) in enumerate((
@@ -121,7 +130,7 @@
         rows[...] = jnp.concatenate(
             [train[...].astype(F32), query[...].astype(F32), jnp.zeros((2, D_IN), F32)], axis=0
         ).astype(BF)
-    pl.semaphore_wait(barrier, 16)
+    pl.semaphore_wait(barrier, 15)
 
     for d in range(1, 8):
         q, peer = row_peer(d)
@@ -257,17 +266,19 @@
         wait(0, 0, 5)
         for b in range(4):
             a_query[pl.ds(b * 128, 128), :] = turned(hi[0, b])
-        wait(1, 0, 6)
-        for b in range(4):
-            for s in range(2):
-                g_query[:, pl.ds(s * 512 + b * 128, 128)] = hg[0, s, b]
-
-    def scale(low, high):
+
+    def scale(half, low, high):
+        if low == 0:
+            if half == 1:
+                wait(1, 0, 6)
+            for b in range(4):
+                g_query[:, pl.ds(half * 512 + b * 128, 128)] = hg[0, (k, other)[half], b]
+
         def body(q, carry):
             inside = (true_rows[...] >= starts[q]) & (true_rows[...] < ends[q])
             rows = jnp.where(inside, a_query[...], 0.0).astype(BF)
-            for o in range(4):
-                at = pl.ds(o * 256, 256)
+            for o in range(2):
+                at = pl.ds(half * 512 + o * 256, 256)
                 outer = jnp.dot(rows, g_query[:, at], preferred_element_type=F32)
                 scaled[q, :, at] = (outer * inverse[:, at]).astype(BF)
             return carry
@@ -281,7 +292,8 @@
         wait(1, c, 6)
         for b in range(4):
             for s in range(2):
-                g_train[c - 1, pl.ds(s * 512 + b * 128, 128), :] = turned(hg[c, s, b]).astype(BF)
+                block = hg[c, (k, other)[s], b]
+                g_train[c - 1, pl.ds(s * 512 + b * 128, 128), :] = turned(block).astype(BF)
 
     def pair(c, low, high):
         def body(q, carry):
@@ -291,30 +303,26 @@
 
         lax.fori_loop(low, high, body, 0, unroll=high - low)
 
-    score_at = (k, z, x, y)
-    score_peer = (lambda d: {"k": other}, z_peer, x_peer, y_peer)
-
-    def share(half, n):
-        if n == 0:
-            value = acc[half]
-        else:
-            value = summed(half, n - 1)
-        stage[half, n, score_at[n]] = value
-        ref = stage.at[half, n, score_at[n]]
-        pair_of = (ssem.at[9 + half], rsem.at[45 + half * 4 + n])
-        if n == 0:
-            moving[half, n] = send(ref, ref, *pair_of, score_peer[n](1))
-        else:
-            for d in range(1, 4):
-                send(ref, ref, *pair_of, score_peer[n](d))
-            moving[half, n] = arrival(stage.at[half, n, 0:3], *pair_of, score_peer[n](1))
-
-    def summed(half, n):
-        wait(half, n)
-        value = stage[half, n, 0] + stage[half, n, 1]
-        if n:
-            value = value + (stage[half, n, 2] + stage[half, n, 3])
-        return value
+    def share_near(half):
+        ref = near_sums.at[half, near]
+        ref[...] = acc[half]
+        pair_of = (ssem.at[9 + half], rsem.at[45 + half])
+        for d in range(1, 8):
+            send(ref, ref, *pair_of, near_peer(d))
+        moving[half, 0] = arrival(near_sums.at[half, 0:7], *pair_of, near_peer(1))
+
+    def share_plane(half):
+        wait(half, 0)
+        ref = plane_sums.at[half, plane]
+        ref[...] = tree([near_sums[half, i] for i in range(8)])
+        pair_of = (ssem.at[9 + half], rsem.at[47 + half])
+        for d in range(1, 16):
+            send(ref, ref, *pair_of, plane_peer(d))
+        moving[half, 1] = arrival(plane_sums.at[half, 0:15], *pair_of, plane_peer(1))
+
+    def summed(half):
+        wait(half, 1)
+        return tree([plane_sums[half, i] for i in range(16)])
 
     def in_order(value, half):
         total = 0.0
@@ -343,38 +351,36 @@
     swap(0)
     rotate(0)
     swap(1)
+    swap(2)
     rotate(1)
-    swap(2)
+    reduce_y(0)
     rotate(2)
     local[6].wait()
-    inverse[...] = jnp.transpose(1.0 / (eig[...] + damping), (1, 0))
-    reduce_y(0)
+    for half, at in enumerate((k, other)):
+        rows = eig[pl.ds(pl.multiple_of(at * 512, 512), 512), :]
+        inverse[:, pl.ds(half * 512, 512)] = jnp.transpose(1.0 / (rows + damping), (1, 0))
+    spread(0)
     reduce_y(1)
-    spread(0)
     reduce_y(2)
     spread(1)
-    spread(2)
     spread_core(0)
     lay_query()
-    scale(0, 8)
+    scale(0, 0, 16)
+    spread(2)
+    scale(1, 0, 8)
     spread_core(1)
+    scale(1, 8, 16)
     spread_core(2)
-    scale(8, 16)
     lay_train(1)
     pair(1, 0, 16)
-    share(0, 0)
+    share_near(0)
     lay_train(2)
-    pair(2, 0, 8)
-    share(0, 1)
-    pair(2, 8, 16)
-    share(1, 0)
-    share(0, 2)
-    share(1, 1)
-    share(0, 3)
-    share(1, 2)
-    early = in_order(summed(0, 3), 0)
-    share(1, 3)
-    total = early + in_order(summed(1, 3), 1)
+    pair(2, 0, 16)
+    share_near(1)
+    share_plane(0)
+    share_plane(1)
+    early = in_order(summed(0), 0)
+    total = early + in_order(summed(1), 1)
     out[...] = total * (1.0 / math.sqrt(D_IN * D_OUT * QBLOCK))
 
 
@@ -435,10 +441,11 @@
             pltpu.VMEM((128, 128), BF),
             pltpu.VMEM((2, 256, 512), BF),
             pltpu.VMEM((1, 256), jnp.int32),
-            pltpu.VMEM((2, 4, 4, NQ, 256), F32),
+            pltpu.VMEM((2, 8, NQ, 256), F32),
+            pltpu.VMEM((2, 16, NQ, 256), F32),
             pltpu.SemaphoreType.DMA((7,)),
             pltpu.SemaphoreType.DMA((11,)),
-            pltpu.SemaphoreType.DMA((53,)),
+            pltpu.SemaphoreType.DMA((49,)),
         ],
         compiler_params=pltpu.CompilerParams(
             collective_id=0, has_side_effects=True, vmem_limit_bytes=56 * 2**20

time: 79 us -> 73.1 us (0.925)
  Pallas kernels: 77.5 us -> 71.5 us
    pallas_call x1, Pallas kernels: 77.5 us -> 71.5 us  [shards(): pl.pallas_call(kernel, out_shape=jax.ShapeDtypeStruct((NQ, 512), F32), in...]
where the time goes in v5:
time: 73.1 us; the launch traced here: 72.9 us
  Pallas kernels  71.5 us (98%)
  local copies, waits for them, and re-layouts  1.38 us (2%)
    pallas_call x1, Pallas kernels, shards(): pl.pallas_call(kernel, out_shape=jax.ShapeDtypeStruct((NQ, 512), F32), in...  71.5 us

profile of v5, /device:TPU:0, one launch (start us, length us, event | category | flops | bytes accessed | tf_op | source)
XLA Modules:
  0.0 72.9 jit_solution(17842145786403854689)
XLA Ops:
  0.0 71.5 %shard_map.91 = f32[16,512]{1,0:T(8,128)} custom-call(s32[16]{0:T(128)} %starts.1, s32[16]{0:T(128)} %ends.1, bf16[4,8192]{1,0:T(4,128)(2,1)} %ti.1, bf16[2,8192]{1,0:T(2,128)(2,1)} %qi.1, bf16[4,8192]{1,0:T(4,128)(2,1)} %tg.1, bf16[2,8192]{1,0:T(2,128)(2,1)} %qg.1, bf16[1024,512]{1,0:T(8,128)(2,1)} %bi_hbm.1, bf16[512,1024]{1,0:T(8,128)(2,1)} %bo_hbm.1, ...), custom_call_target="tpu_custom_call" | custom-call | tf_op jit(solution)/shard_map/pallas_call | solution.py:400
  71.5 1.4 %copy.11 = f32[16,512]{1,0:T(8,128)} copy(f32[16,512]{1,0:T(8,128)} %shard_map.91) | data formatting | bytes 65536

commit v6 on v5

--- a/solution.py
+++ b/solution.py
@@ -303,26 +303,32 @@
 
         lax.fori_loop(low, high, body, 0, unroll=high - low)
 
-    def share_near(half):
-        ref = near_sums.at[half, near]
-        ref[...] = acc[half]
-        pair_of = (ssem.at[9 + half], rsem.at[45 + half])
+    pieces = ((0, 0, 16), (1, 0, 8), (1, 8, 8))
+
+    def share_near(i):
+        half, low, size = pieces[i]
+        rows = pl.ds(0, size)
+        near_sums[i, near, rows, :] = acc[half, pl.ds(low, size), :]
+        ref = near_sums.at[i, near, rows]
+        pair_of = (ssem.at[9 + i], rsem.at[45 + i])
         for d in range(1, 8):
             send(ref, ref, *pair_of, near_peer(d))
-        moving[half, 0] = arrival(near_sums.at[half, 0:7], *pair_of, near_peer(1))
-
-    def share_plane(half):
-        wait(half, 0)
-        ref = plane_sums.at[half, plane]
-        ref[...] = tree([near_sums[half, i] for i in range(8)])
-        pair_of = (ssem.at[9 + half], rsem.at[47 + half])
+        moving["near", i] = arrival(near_sums.at[i, 0:7, rows], *pair_of, near_peer(1))
+
+    def share_plane(i):
+        wait("near", i)
+        rows = pl.ds(0, pieces[i][2])
+        plane_sums[i, plane, rows, :] = tree([near_sums[i, j, rows, :] for j in range(8)])
+        ref = plane_sums.at[i, plane, rows]
+        pair_of = (ssem.at[9 + i], rsem.at[48 + i])
         for d in range(1, 16):
             send(ref, ref, *pair_of, plane_peer(d))
-        moving[half, 1] = arrival(plane_sums.at[half, 0:15], *pair_of, plane_peer(1))
-
-    def summed(half):
-        wait(half, 1)
-        return tree([plane_sums[half, i] for i in range(16)])
+        moving["plane", i] = arrival(plane_sums.at[i, 0:15, rows], *pair_of, plane_peer(1))
+
+    def summed(i):
+        wait("plane", i)
+        rows = pl.ds(0, pieces[i][2])
+        return tree([plane_sums[i, j, rows, :] for j in range(16)])
 
     def in_order(value, half):
         total = 0.0
@@ -362,25 +368,30 @@
     spread(0)
     reduce_y(1)
     reduce_y(2)
-    spread(1)
     spread_core(0)
     lay_query()
-    scale(0, 0, 16)
+    spread(1)
+    scale(0, 0, 8)
     spread(2)
-    scale(1, 0, 8)
+    scale(0, 8, 16)
+    scale(1, 0, 16)
     spread_core(1)
-    scale(1, 8, 16)
+    lay_train(1)
+    pair(1, 0, 8)
     spread_core(2)
-    lay_train(1)
-    pair(1, 0, 16)
+    pair(1, 8, 16)
     share_near(0)
     lay_train(2)
-    pair(2, 0, 16)
+    pair(2, 0, 8)
     share_near(1)
+    pair(2, 8, 16)
+    share_near(2)
     share_plane(0)
     share_plane(1)
     early = in_order(summed(0), 0)
-    total = early + in_order(summed(1), 1)
+    share_plane(2)
+    late = in_order(jnp.concatenate([summed(1), summed(2)], axis=0), 1)
+    total = early + late
     out[...] = total * (1.0 / math.sqrt(D_IN * D_OUT * QBLOCK))
 
 
@@ -441,11 +452,11 @@
             pltpu.VMEM((128, 128), BF),
             pltpu.VMEM((2, 256, 512), BF),
             pltpu.VMEM((1, 256), jnp.int32),
-            pltpu.VMEM((2, 8, NQ, 256), F32),
-            pltpu.VMEM((2, 16, NQ, 256), F32),
+            pltpu.VMEM((3, 8, NQ, 256), F32),
+            pltpu.VMEM((3, 16, NQ, 256), F32),
             pltpu.SemaphoreType.DMA((7,)),
-            pltpu.SemaphoreType.DMA((11,)),
-            pltpu.SemaphoreType.DMA((49,)),
+            pltpu.SemaphoreType.DMA((12,)),
+            pltpu.SemaphoreType.DMA((51,)),
         ],
         compiler_params=pltpu.CompilerParams(
             collective_id=0, has_side_effects=True, vmem_limit_bytes=56 * 2**20

time: 73.1 us -> 74.5 us (1.019)
  Pallas kernels: 71.5 us -> 72.9 us
    pallas_call x1, Pallas kernels: 71.5 us -> 72.9 us  [shards(): pl.pallas_call(kernel, out_shape=jax.ShapeDtypeStruct((NQ, 512), F32), in...]
where the time goes in v6:
time: 74.5 us; the launch traced here: 74.3 us
  Pallas kernels  72.9 us (98%)
  local copies, waits for them, and re-layouts  1.38 us (2%)
    pallas_call x1, Pallas kernels, shards(): pl.pallas_call(kernel, out_shape=jax.ShapeDtypeStruct((NQ, 512), F32), in...  72.9 us

profile of v6, /device:TPU:0, one launch (start us, length us, event | category | flops | bytes accessed | tf_op | source)
XLA Modules:
  0.0 74.3 jit_solution(6155267905568803927)
XLA Ops:
  0.0 72.9 %shard_map.91 = f32[16,512]{1,0:T(8,128)} custom-call(s32[16]{0:T(128)} %starts.1, s32[16]{0:T(128)} %ends.1, bf16[4,8192]{1,0:T(4,128)(2,1)} %ti.1, bf16[2,8192]{1,0:T(2,128)(2,1)} %qi.1, bf16[4,8192]{1,0:T(4,128)(2,1)} %tg.1, bf16[2,8192]{1,0:T(2,128)(2,1)} %qg.1, bf16[1024,512]{1,0:T(8,128)(2,1)} %bi_hbm.1, bf16[512,1024]{1,0:T(8,128)(2,1)} %bo_hbm.1, ...), custom_call_target="tpu_custom_call" | custom-call | tf_op jit(solution)/shard_map/pallas_call | solution.py:411
  72.9 1.4 %copy.11 = f32[16,512]{1,0:T(8,128)} copy(f32[16,512]{1,0:T(8,128)} %shard_map.91) | data formatting | bytes 65536

commit v7 on v6

--- a/solution.py
+++ b/solution.py
@@ -192,7 +192,7 @@
     def gather_xz(side, c):
         wait(side, c, 0)
         ref = gathered[side].at[c, k, gather_at[side][0]]
-        for d in range(1, 4):
+        for d in (2, 1, 3):
             send(ref, ref, *sems(side, c, 1), gather_peer[side](d))
         moving[side, c, 1] = arrival(
             gathered[side].at[c, k, 0:3], *sems(side, c, 1), gather_peer[side](1)
@@ -222,7 +222,7 @@
                     piece = value[:, b * 128 : (b + 1) * 128]
                     part[side][c, b, pl.ds(low, size)] = piece
                     small[side][c, b, pl.ds(low, size)] = piece.astype(BF)
-            for d in range(1, 4):
+            for d in (2, 1, 3):
                 q = lax.rem(sum_at[side] + d, 4)
                 send(
                     small[side].at[c, q], got[side].at[c, d - 1], *sems(side, c, 3),
@@ -253,7 +253,7 @@
             ref = hi.at[c, at] if side == 0 else hg.at[c, k, at]
             ref[...] = (part[side][c, at] + more).astype(BF)
             peer = x_peer if side == 0 else z_peer
-            for d in range(1, 4):
+            for d in (2, 1, 3):
                 send(ref, ref, *sems(side, c, 5), peer(d))
             three = hi.at[c, 0:3] if side == 0 else hg.at[c, k, 0:3]
             moving[side, c, 5] = arrival(three, *sems(side, c, 5), peer(1))
@@ -303,7 +303,7 @@
 
         lax.fori_loop(low, high, body, 0, unroll=high - low)
 
-    pieces = ((0, 0, 16), (1, 0, 8), (1, 8, 8))
+    pieces = ((0, 0, 16), (1, 0, 16))
 
     def share_near(i):
         half, low, size = pieces[i]
@@ -382,16 +382,12 @@
     pair(1, 8, 16)
     share_near(0)
     lay_train(2)
-    pair(2, 0, 8)
+    pair(2, 0, 16)
     share_near(1)
-    pair(2, 8, 16)
-    share_near(2)
     share_plane(0)
     share_plane(1)
-    early = in_order(summed(0), 0)
-    share_plane(2)
-    late = in_order(jnp.concatenate([summed(1), summed(2)], axis=0), 1)
-    total = early + late
+    total = in_order(summed(0), 0)
+    total = total + in_order(summed(1), 1)
     out[...] = total * (1.0 / math.sqrt(D_IN * D_OUT * QBLOCK))
 
 

time: 74.5 us -> 72.4 us (0.972)
  Pallas kernels: 72.9 us -> 70.6 us
    pallas_call x1, Pallas kernels: 72.9 us -> 70.6 us  [shards(): pl.pallas_call(kernel, out_shape=jax.ShapeDtypeStruct((NQ, 512), F32), in...]
where the time goes in v7:
time: 72.4 us; the launch traced here: 71.9 us
  Pallas kernels  70.6 us (98%)
  local copies, waits for them, and re-layouts  1.38 us (2%)
    pallas_call x1, Pallas kernels, shards(): pl.pallas_call(kernel, out_shape=jax.ShapeDtypeStruct((NQ, 512), F32), in...  70.6 us

profile of v7, /device:TPU:0, one launch (start us, length us, event | category | flops | bytes accessed | tf_op | source)
XLA Modules:
  0.0 71.9 jit_solution(7594981094847516895)
XLA Ops:
  0.0 70.6 %shard_map.91 = f32[16,512]{1,0:T(8,128)} custom-call(s32[16]{0:T(128)} %starts.1, s32[16]{0:T(128)} %ends.1, bf16[4,8192]{1,0:T(4,128)(2,1)} %ti.1, bf16[2,8192]{1,0:T(2,128)(2,1)} %qi.1, bf16[4,8192]{1,0:T(4,128)(2,1)} %tg.1, bf16[2,8192]{1,0:T(2,128)(2,1)} %qg.1, bf16[1024,512]{1,0:T(8,128)(2,1)} %bi_hbm.1, bf16[512,1024]{1,0:T(8,128)(2,1)} %bo_hbm.1, ...), custom_call_target="tpu_custom_call" | custom-call | tf_op jit(solution)/shard_map/pallas_call | solution.py:407
  70.6 1.4 %copy.11 = f32[16,512]{1,0:T(8,128)} copy(f32[16,512]{1,0:T(8,128)} %shard_map.91) | data formatting | bytes 65536

commit v8 on v7

--- a/solution.py
+++ b/solution.py
@@ -374,8 +374,9 @@
     scale(0, 0, 8)
     spread(2)
     scale(0, 8, 16)
-    scale(1, 0, 16)
+    scale(1, 0, 8)
     spread_core(1)
+    scale(1, 8, 16)
     lay_train(1)
     pair(1, 0, 8)
     spread_core(2)

time: 72.4 us -> 72.1 us (level)
  no operation moved by 1% of the time
where the time goes in v8:
time: 72.1 us; the launch traced here: 71.8 us
  Pallas kernels  70.4 us (98%)
  local copies, waits for them, and re-layouts  1.38 us (2%)
    pallas_call x1, Pallas kernels, shards(): pl.pallas_call(kernel, out_shape=jax.ShapeDtypeStruct((NQ, 512), F32), in...  70.4 us

profile of v8, /device:TPU:0, one launch (start us, length us, event | category | flops | bytes accessed | tf_op | source)
XLA Modules:
  0.0 71.8 jit_solution(9172677320495125566)
XLA Ops:
  0.0 70.4 %shard_map.91 = f32[16,512]{1,0:T(8,128)} custom-call(s32[16]{0:T(128)} %starts.1, s32[16]{0:T(128)} %ends.1, bf16[4,8192]{1,0:T(4,128)(2,1)} %ti.1, bf16[2,8192]{1,0:T(2,128)(2,1)} %qi.1, bf16[4,8192]{1,0:T(4,128)(2,1)} %tg.1, bf16[2,8192]{1,0:T(2,128)(2,1)} %qg.1, bf16[1024,512]{1,0:T(8,128)(2,1)} %bi_hbm.1, bf16[512,1024]{1,0:T(8,128)(2,1)} %bo_hbm.1, ...), custom_call_target="tpu_custom_call" | custom-call | tf_op jit(solution)/shard_map/pallas_call | solution.py:408
  70.4 1.4 %copy.11 = f32[16,512]{1,0:T(8,128)} copy(f32[16,512]{1,0:T(8,128)} %shard_map.91) | data formatting | bytes 65536
